TPU v7x, 256 devices: a whole 4x4x8 slice. The times are simulated.
256 devices in a mesh: dp: 16 (over y, x_hi, core), mp: 16 (over z, x_lo).
Axes of the slice: x: 4 (x_hi: 2, x_lo: 2; x = x_hi * 2 + x_lo), y: 4, z: 8, core: 2. Of those that a mesh axis runs over, the one named last changes fastest.
Arguments:
- tokens: bfloat16 [16384, 2048], P(('dp', 'mp')), may hold values from -6 to 6
- norm_gain: float32 [2048], replicated, may hold values from 0.1 to 1.9
- mlp_gain: float32 [2048], replicated, may hold values from 0.1 to 1.9
- lengths: int32 [16], P('dp'), may hold values from 1 to 1024, as said below
- log_decay: float32 [16384, 8], P('dp'), as said below
- query_master: float32 [2048, 2048], P(('dp', 'mp')), may hold values from -0.125 to 0.125
- key_master: float32 [2048, 2048], P(('dp', 'mp')), may hold values from -0.125 to 0.125
- value_master: float32 [2048, 4096], P(('dp', 'mp')), may hold values from -0.125 to 0.125
- swish_master: float32 [2048, 4096], P(('dp', 'mp')), may hold values from -0.125 to 0.125
- output_master: float32 [4096, 2048], P(None, ('dp', 'mp')), may hold values from -0.09375 to 0.09375
- ffn_gate_master: float32 [2048, 4096], P(('dp', 'mp')), may hold values from -0.125 to 0.125
- ffn_up_master: float32 [2048, 4096], P(('dp', 'mp')), may hold values from -0.125 to 0.125
Outputs:
- residual: bfloat16 [16384, 2048], P(('dp', 'mp'))
- hidden: bfloat16 [16384, 4096], P('dp', 'mp')
Inputs may be any that keep to these rules, and one draw needn't show every extreme that they name: `lengths`: given length of each prompt; in every draw some prompt has exactly 1024 tokens and some has 1. `log_decay`: Negative.
All inputs are finite; a program needn't handle non-finite values.
Results may differ from a plain program's by a relative error of at most 0.023.
Values may be sent and summed in bfloat16 or wider, within the bound.
A program may use at most 128 MiB of HBM per device.

v0:
```python
import math

import jax
import jax.numpy as jnp
from jax import lax
from jax.sharding import PartitionSpec as P

H = 8
DK = 256
DV = 512
REQUEST_SPAN = 1024
BLOCK = 512
PROMPTS_DP = 1


def rms_rows(row_block, gain_vec):
    values = row_block.astype(jnp.float32)
    scale = lax.rsqrt(jnp.mean(values * values, axis=-1, keepdims=True) + 1e-06)
    return (values * scale * gain_vec).astype(jnp.bfloat16)


def rotate(values, places):
    columns = values.shape[1]
    channel = jnp.arange(columns, dtype=jnp.int32) % DK
    paired = (channel // 2 * 2).astype(jnp.float32)
    frequency = jnp.exp(paired * (-math.log(10000.0) / DK))
    angles = places.astype(jnp.float32)[:, None] * frequency[None, :]
    couples = values.reshape(values.shape[0], columns // 2, 2)
    turned = jnp.stack([-couples[:, :, 1], couples[:, :, 0]], axis=-1).reshape(values.shape)
    return values * jnp.cos(angles) + turned * jnp.sin(angles)


def spread_heads(matrix, width, copies):
    row_total = matrix.shape[0]
    per_head = jnp.repeat(matrix.reshape(row_total, H, width), copies, axis=1)
    return per_head.reshape(row_total, H * copies * width)


def trainer_order(block_rows, dp_count, mp_count):
    row_total, columns = block_rows.shape
    split_rows = block_rows.reshape(mp_count, dp_count, row_total // (dp_count * mp_count), columns)
    return split_rows.transpose(1, 0, 2, 3).reshape(row_total, columns)


def retain_block(offset, q_block, k_block, v_block, run_query, run_key):
    scores = jnp.einsum(
        "thd,shd->hts", q_block, k_block, preferred_element_type=jnp.float32
    ) * DK ** (-0.5)
    decay_gap = run_query.T[:, :, None] - run_key.T[:, None, :]
    causal_mask = (offset + jnp.arange(q_block.shape[0], dtype=jnp.int32))[:, None] >= jnp.arange(
        k_block.shape[0], dtype=jnp.int32
    )[None, :]
    weights = (scores * jnp.exp(jnp.where(causal_mask[None], decay_gap, -jnp.inf))).astype(
        jnp.bfloat16
    )
    return jnp.einsum("hts,shd->thd", weights, v_block, preferred_element_type=jnp.float32)


def per_device(
    tokens,
    norm_gain,
    mlp_gain,
    lengths,
    log_decay,
    query_master,
    key_master,
    value_master,
    swish_master,
    output_master,
    ffn_gate_master,
    ffn_up_master,
):
    mp_count = lax.axis_size("mp")
    dp_count = lax.axis_size("dp")
    mp_index = lax.axis_index("mp")
    head_share = max(1, mp_count // H)
    local_heads = max(1, H // mp_count)
    partner_bit = mp_index % head_share
    group_rows = PROMPTS_DP * REQUEST_SPAN
    value_width = DV // head_share
    m_query = spread_heads(query_master.astype(jnp.bfloat16), DK, head_share)
    m_key = spread_heads(key_master.astype(jnp.bfloat16), DK, head_share)
    m_value = spread_heads(value_master.astype(jnp.bfloat16), DV, head_share)
    m_swish = swish_master.astype(jnp.bfloat16)
    m_output = output_master.T.astype(jnp.bfloat16)
    m_ffn_gate = ffn_gate_master.astype(jnp.bfloat16)
    m_ffn_up = ffn_up_master.astype(jnp.bfloat16)
    r_query, r_key, r_value, r_swish, r_output, r_gate, r_up = (
        lax.all_gather(m_query, "dp", axis=0, tiled=True),
        lax.all_gather(m_key, "dp", axis=0, tiled=True),
        lax.all_gather(m_value, "dp", axis=0, tiled=True),
        lax.all_gather(m_swish, "dp", axis=0, tiled=True),
        lax.all_gather(m_output, "dp", axis=0, tiled=True),
        lax.all_gather(m_ffn_gate, "dp", axis=0, tiled=True),
        lax.all_gather(m_ffn_up, "dp", axis=0, tiled=True),
    )
    owned_parts = (
        lax.all_to_all(r_query, "mp", split_axis=1, concat_axis=0, tiled=True),
        lax.all_to_all(r_key, "mp", split_axis=1, concat_axis=0, tiled=True),
        lax.all_to_all(r_value, "mp", split_axis=1, concat_axis=0, tiled=True),
        lax.all_to_all(r_swish, "mp", split_axis=1, concat_axis=0, tiled=True),
        lax.all_to_all(r_output, "mp", split_axis=1, concat_axis=0, tiled=True),
        lax.all_to_all(r_gate, "mp", split_axis=1, concat_axis=0, tiled=True),
        lax.all_to_all(r_up, "mp", split_axis=1, concat_axis=0, tiled=True),
    )
    server = [trainer_order(owned, dp_count, mp_count) for owned in owned_parts]
    w_query, w_key, w_value, w_swish, w_output, w_ffn_gate, w_ffn_up = server
    width_qk = w_query.shape[1]
    width_value = w_value.shape[1]
    merged_weights = jnp.concatenate([w_query, w_key, w_value, w_swish], axis=1)
    normed_in = rms_rows(tokens, norm_gain)
    shard_piece = lax.all_gather(normed_in, "mp", axis=0, tiled=True)
    places = jnp.arange(shard_piece.shape[0], dtype=jnp.int32) % REQUEST_SPAN
    projected_rows = jnp.dot(shard_piece, merged_weights, preferred_element_type=jnp.float32)
    rotated_query = rotate(projected_rows[:, :width_qk], places)
    rotated_key = rotate(projected_rows[:, width_qk : 2 * width_qk], places)
    projected = jnp.concatenate(
        [rotated_query, rotated_key, projected_rows[:, 2 * width_qk :]], axis=1
    ).astype(jnp.bfloat16)
    queries = projected[:, :width_qk]
    key_rows = projected[:, width_qk : 2 * width_qk]
    value_rows = projected[:, 2 * width_qk : 2 * width_qk + width_value]
    gate_rows = projected[:, 2 * width_qk + width_value :]
    head_first = mp_index // head_share * local_heads
    decay_cols = lax.dynamic_slice_in_dim(log_decay, head_first, local_heads, 1)
    running = jnp.cumsum(decay_cols.reshape(PROMPTS_DP, REQUEST_SPAN, local_heads), axis=1)
    query_four = queries.reshape(PROMPTS_DP, REQUEST_SPAN, local_heads, DK)
    key_four = key_rows.reshape(PROMPTS_DP, REQUEST_SPAN, local_heads, DK)
    value_four = value_rows.reshape(PROMPTS_DP, REQUEST_SPAN, local_heads, DV)

    def one_prompt(prompt_items):
        q_prompt, k_prompt, v_prompt, run_prompt, length_prompt = prompt_items
        outputs = []
        for block_index in range(REQUEST_SPAN // BLOCK):
            low_row = block_index * BLOCK
            top_row = low_row + BLOCK
            operands = (
                q_prompt[low_row:top_row],
                k_prompt[:top_row],
                v_prompt[:top_row],
                run_prompt[low_row:top_row],
                run_prompt[:top_row],
            )
            block_out = retain_block(low_row, *operands)
            outputs.append(block_out)
        return jnp.concatenate(outputs, axis=0)

    retained = lax.map(one_prompt, (query_four, key_four, value_four, running, lengths))
    retained = retained.reshape(group_rows, local_heads, DV)
    channel_mean = jnp.mean(retained, axis=-1, keepdims=True)
    spread = jnp.mean(retained * retained, axis=-1, keepdims=True) - channel_mean * channel_mean
    normed_heads = (retained - channel_mean) * lax.rsqrt(spread + 1e-05)
    normed_heads = lax.dynamic_slice_in_dim(normed_heads, partner_bit * value_width, value_width, 2)
    live_rows = jnp.arange(group_rows, dtype=jnp.int32) % REQUEST_SPAN < jnp.repeat(
        lengths, REQUEST_SPAN
    )
    gated = jnp.where(
        live_rows[:, None],
        jax.nn.silu(gate_rows.astype(jnp.float32))
        * normed_heads.reshape(group_rows, local_heads * value_width),
        0.0,
    ).astype(jnp.bfloat16)
    branch = lax.psum_scatter(
        lax.dot_general(
            gated, w_output, (((1,), (1,)), ((), ())), preferred_element_type=jnp.float32
        ).astype(jnp.bfloat16),
        "mp",
        scatter_dimension=0,
        tiled=True,
    ).astype(jnp.float32)
    residual = (tokens.astype(jnp.float32) + branch).astype(jnp.bfloat16)
    normed_mid = rms_rows(residual, mlp_gain)
    w_gate_up = jnp.concatenate([w_ffn_gate, w_ffn_up], axis=1)
    split_at = w_ffn_gate.shape[1]
    gate_up = jnp.dot(
        lax.all_gather(normed_mid, "mp", axis=0, tiled=True),
        w_gate_up,
        preferred_element_type=jnp.float32,
    )
    hidden = (jax.nn.silu(gate_up[:, :split_at]) * gate_up[:, split_at:]).astype(jnp.bfloat16)
    return (residual, hidden)


def solution(mesh):
    placed = (
        P(("dp", "mp"), None),
        P(),
        P(),
        P("dp"),
        P("dp", None),
        P(("dp", "mp"), None),
        P(("dp", "mp"), None),
        P(("dp", "mp"), None),
        P(("dp", "mp"), None),
        P(None, ("dp", "mp")),
        P(("dp", "mp"), None),
        P(("dp", "mp"), None),
    )
    return jax.shard_map(
        per_device,
        mesh=mesh,
        in_specs=placed,
        out_specs=(P(("dp", "mp"), None), P("dp", "mp")),
        check_vma=False,
    )
```

profile of v0, /device:TPU:1, one launch (start us, length us, event | category | flops | bytes accessed | tf_op | source)
XLA Modules:
  0.0 776.2 jit_solution(15187290181166123529)
XLA Ops:
  13.5 52.0 %all-gather.14.cloned.1.call-done = bf16[128,4096]{1,0:T(8,128)(2,1)} async-done(((bf16[8,4096]{1,0:T(8,128)(2,1)}), bf16[128,4096]{1,0:T(8,128)(2,1)}) %all-gather.14.cloned.1.call-update) | async-done | bytes 1048592 | tf_op jit(solution)/shard_map/all_gather | solution.py:90
  67.8 6.8 all-to-all-start.1
  75.4 41.6 %all-gather.12.cloned.1.call-done = bf16[128,4096]{1,0:T(8,128)(2,1)} async-done(((bf16[8,4096]{1,0:T(8,128)(2,1)}), bf16[128,4096]{1,0:T(8,128)(2,1)}) %all-gather.12.cloned.1.call-update) | async-done | bytes 1048592 | tf_op jit(solution)/shard_map/all_gather | solution.py:89
  119.3 6.8 all-to-all-start
  126.3 42.8 %all-gather.18.cloned.1.call-done = bf16[128,4096]{1,0:T(8,128)(2,1)} async-done(((bf16[8,4096]{1,0:T(8,128)(2,1)}), bf16[128,4096]{1,0:T(8,128)(2,1)}) %all-gather.18.cloned.1.call-update) | async-done | bytes 1048592 | tf_op jit(solution)/shard_map/all_gather | solution.py:92
  171.4 6.8 all-to-all-start.3
  179.1 41.3 %all-gather.20.cloned.1.call-done = bf16[128,4096]{1,0:T(8,128)(2,1)} async-done(((bf16[8,4096]{1,0:T(8,128)(2,1)}), bf16[128,4096]{1,0:T(8,128)(2,1)}) %all-gather.20.cloned.1.call-update) | async-done | bytes 1048592 | tf_op jit(solution)/shard_map/all_gather | solution.py:93
  222.7 6.9 all-to-all-start.4
  229.6 45.4 %all-gather.16.cloned.1.call-done = bf16[128,8192]{1,0:T(8,128)(2,1)} async-done(((bf16[8,8192]{1,0:T(8,128)(2,1)}), bf16[128,8192]{1,0:T(8,128)(2,1)}) %all-gather.16.cloned.1.call-update) | async-done | bytes 2097168 | tf_op jit(solution)/shard_map/all_gather | solution.py:91
  275.0 4.1 copy.69
  279.1 6.8 all-to-all-start.2
  301.4 49.0 %all-to-all-done.2 = bf16[128,16,512]{0,2,1:T(8,128)(2,1)S(1)} async-done(((bf16[128,16,512]{0,2,1:T(8,128)(2,1)}), bf16[128,16,512]{0,2,1:T(8,128)(2,1)S(1)}, u32[]{:S(2)}, u32[]{:S(2)}) %all-to-all-start.2) | async-done | bytes 2097184 | tf_op jit(solution)/shard_map/all_to_all | solution.py:100
  354.9 52.4 %all-gather.10.cloned.1.call-done = bf16[1024,2048]{1,0:T(8,128)(2,1)} async-done(((bf16[64,2048]{1,0:T(8,128)(2,1)}), bf16[1024,2048]{1,0:T(8,128)(2,1)}) %all-gather.10.cloned.1.call-update) | async-done | bytes 4194320 | tf_op jit(solution)/shard_map/all_gather | solution.py:112
  407.3 9.9 %fusion.85 = (bf16[1024,1280]{1,0:T(8,128)(2,1)}, f32[1024,1280]{1,0:T(8,128)S(1)}) fusion(bf16[1024,2048]{1,0:T(8,128)(2,1)} %all-gather.10.cloned.1.call-done, bf16[2048,256]{1,0:T(8,128)(2,1)} %bitcast.111, bf16[2048,512]{1,0:T(8,128)(2,1)S(1)} %bitcast.107, bf16[2048,256]{1,0:T(8,128)(2,1)S(1)} %bitcast.109, bf16[2048,256]{1,0:T(8,128)(2,1)} %bitcast.110), kind=kOutput, calls=%fused_computation.126 | convolution fusion | flops 5390991360 | bytes 17301504 | tf_op jit(solution)/shard_map/dot_general | solution.py:114
  428.7 7.1 fusion.25
  441.5 4.5 convolution_convert_fusion
  448.4 96.5 %reduce-scatter.2.cloned.1.call-done = bf16[64,2048]{1,0:T(8,128)(2,1)} async-done(((bf16[1024,2048]{1,0:T(8,128)(2,1)}), bf16[64,2048]{1,0:T(8,128)(2,1)}) %reduce-scatter.2.cloned.1.call-update) | async-done | bytes 262160 | tf_op jit(solution)/shard_map/reduce_scatter | solution.py:163
  546.9 52.9 %all-gather.24.cloned.1.call-done = bf16[128,4096]{1,0:T(8,128)(2,1)} async-done(((bf16[8,4096]{1,0:T(8,128)(2,1)}), bf16[128,4096]{1,0:T(8,128)(2,1)}) %all-gather.24.cloned.1.call-update) | async-done | bytes 1048592 | tf_op jit(solution)/shard_map/all_gather | solution.py:94
  602.1 6.8 all-to-all-start.5
  608.9 42.4 %all-gather.26.cloned.1.call-done = bf16[128,4096]{1,0:T(8,128)(2,1)} async-done(((bf16[8,4096]{1,0:T(8,128)(2,1)}), bf16[128,4096]{1,0:T(8,128)(2,1)}) %all-gather.26.cloned.1.call-update) | async-done | bytes 1048592 | tf_op jit(solution)/shard_map/all_gather | solution.py:95
  653.6 6.8 all-to-all-start.6
  662.1 31.7 %all-to-all-done.6 = bf16[128,16,256]{0,2,1:T(8,128)(2,1)S(1)} async-done(((bf16[128,16,256]{0,2,1:T(8,128)(2,1)}), bf16[128,16,256]{0,2,1:T(8,128)(2,1)S(1)}, u32[]{:S(2)}, u32[]{:S(2)}) %all-to-all-start.6) | async-done | bytes 1048608 | tf_op jit(solution)/shard_map/all_to_all | solution.py:104
  694.4 69.3 %all-gather.22.cloned.1.call-done = bf16[1024,2048]{1,0:T(8,128)(2,1)} async-done(((bf16[64,2048]{1,0:T(8,128)(2,1)}), bf16[1024,2048]{1,0:T(8,128)(2,1)}) %all-gather.22.cloned.1.call-update) | async-done | bytes 4194320 | tf_op jit(solution)/shard_map/all_gather | solution.py:176
  763.7 4.5 fusion.8
  (131 shorter events, 65.7 us)
Async XLA Ops:
  7.2 278.9 %copy-start = (f32[1024,8]{0,1:T(8,128)S(1)}, f32[1024,8]{0,1:T(8,128)}, u32[]{:S(2)}) copy-start(f32[1024,8]{0,1:T(8,128)} %param.16) | copy-start | bytes 98308
  7.2 67.5 %copy-start.14 = (f32[8,4096]{1,0:T(8,128)S(1)}, f32[8,4096]{1,0:T(8,128)}, u32[]{:S(2)}) copy-start(f32[8,4096]{1,0:T(8,128)} %param.19) | copy-start | bytes 393220
  7.2 58.3 %all-gather.14.cloned.1.call-start = ((), (), s32[]{:S(2)}) async-start(), calls=%async_computation.10 | async-start | bytes 1114112 | tf_op jit(solution)/shard_map/all_gather | solution.py:90
  8.8 108.2 %all-gather.12.cloned.1.call-start = ((), (), s32[]{:S(2)}) async-start(), calls=%async_computation.9 | async-start | bytes 1114112 | tf_op jit(solution)/shard_map/all_gather | solution.py:89
  10.3 158.7 %all-gather.18.cloned.1.call-start = ((), (), s32[]{:S(2)}) async-start(), calls=%async_computation.12 | async-start | bytes 1114112 | tf_op jit(solution)/shard_map/all_gather | solution.py:92
  11.9 208.5 %all-gather.20.cloned.1.call-start = ((), (), s32[]{:S(2)}) async-start(), calls=%async_computation.13 | async-start | bytes 1114112 | tf_op jit(solution)/shard_map/all_gather | solution.py:93
  67.8 51.5 %all-to-all-start.1 = ((bf16[128,16,256]{0,2,1:T(8,128)(2,1)}), bf16[128,16,256]{0,2,1:T(8,128)(2,1)S(1)}, u32[]{:S(2)}, u32[]{:S(2)}) async-start(bf16[128,16,256]{0,2,1:T(8,128)(2,1)} %bitcast.10), calls=%async_computation.1 | async-start | bytes 2097152 | tf_op jit(solution)/shard_map/all_to_all | solution.py:99
  74.7 200.4 %all-gather.16.cloned.1.call-start = ((), (), s32[]{:S(2)}) async-start(), calls=%async_computation.11 | async-start | bytes 2228224 | tf_op jit(solution)/shard_map/all_gather | solution.py:91
  119.3 52.1 %all-to-all-start = ((bf16[128,16,256]{0,2,1:T(8,128)(2,1)}), bf16[128,16,256]{0,2,1:T(8,128)(2,1)S(1)}, u32[]{:S(2)}, u32[]{:S(2)}) async-start(bf16[128,16,256]{0,2,1:T(8,128)(2,1)} %bitcast.3), calls=%async_computation | async-start | bytes 2097152 | tf_op jit(solution)/shard_map/all_to_all | solution.py:98
  171.4 51.3 %all-to-all-start.3 = ((bf16[128,16,256]{0,2,1:T(8,128)(2,1)}), bf16[128,16,256]{0,2,1:T(8,128)(2,1)S(1)}, u32[]{:S(2)}, u32[]{:S(2)}) async-start(bf16[128,16,256]{0,2,1:T(8,128)(2,1)} %bitcast.97), calls=%async_computation.3 | async-start | bytes 2097152 | tf_op jit(solution)/shard_map/all_to_all | solution.py:101
  178.2 229.1 %all-gather.10.cloned.1.call-start = ((), (), s32[]{:S(2)}) async-start(), calls=%async_computation.8 | async-start | bytes 4456448 | tf_op jit(solution)/shard_map/all_gather | solution.py:112
  222.7 56.5 %copy-start.4 = (bf16[128,16,256]{0,2,1:T(8,128)(2,1)}, bf16[128,16,256]{0,2,1:T(8,128)(2,1)S(1)}, u32[]{:S(2)}) copy-start(bf16[128,16,256]{0,2,1:T(8,128)(2,1)S(1)} %all-to-all-done.3) | copy-start | bytes 3145732
  222.7 56.5 %all-to-all-start.4 = ((bf16[128,16,256]{0,2,1:T(8,128)(2,1)}), bf16[128,16,256]{0,2,1:T(8,128)(2,1)}, u32[]{:S(2)}, u32[]{:S(2)}) async-start(bf16[128,16,256]{0,2,1:T(8,128)(2,1)} %bitcast.99), calls=%async_computation.4 | async-start | bytes 2097152 | tf_op jit(solution)/shard_map/all_to_all | solution.py:102
  279.1 71.3 %all-to-all-start.2 = ((bf16[128,16,512]{0,2,1:T(8,128)(2,1)}), bf16[128,16,512]{0,2,1:T(8,128)(2,1)S(1)}, u32[]{:S(2)}, u32[]{:S(2)}) async-start(bf16[128,16,512]{0,2,1:T(8,128)(2,1)} %bitcast.17), calls=%async_computation.2 | async-start | bytes 4194304 | tf_op jit(solution)/shard_map/all_to_all | solution.py:100
  286.0 258.9 %reduce-scatter.2.cloned.1.call-start = ((), (), s32[]{:S(2)}) async-start(), calls=%async_computation.14 | async-start | bytes 4456448 | tf_op jit(solution)/shard_map/reduce_scatter | solution.py:163
  353.0 54.3 %copy-start.9 = (bf16[16,16,8,256]{3,2,1,0:T(8,128)(2,1)S(1)}, bf16[16,16,8,256]{3,2,1,0:T(8,128)(2,1)}, u32[]{:S(2)}) copy-start(bf16[16,16,8,256]{3,2,1,0:T(8,128)(2,1)} %copy.68) | copy-start | bytes 3145732
  446.0 100.0 %copy-start.18 = (f32[2048]{0:T(1024)S(1)}, f32[2048]{0:T(1024)}, u32[]{:S(2)}) copy-start(f32[2048]{0:T(1024)} %param.14) | copy-start | bytes 24580
  446.1 153.7 %all-gather.24.cloned.1.call-start = ((), (), s32[]{:S(2)}) async-start(), calls=%async_computation.16 | async-start | bytes 1114112 | tf_op jit(solution)/shard_map/all_gather | solution.py:94
  447.6 203.7 %all-gather.26.cloned.1.call-start = ((), (), s32[]{:S(2)}) async-start(), calls=%async_computation.17 | async-start | bytes 1114112 | tf_op jit(solution)/shard_map/all_gather | solution.py:95
  448.3 315.4 %all-gather.22.cloned.1.call-start = ((), (), s32[]{:S(2)}) async-start(), calls=%async_computation.15 | async-start | bytes 4456448 | tf_op jit(solution)/shard_map/all_gather | solution.py:176
  546.0 56.1 %copy-start.11 = (bf16[64,2048]{1,0:T(8,128)(2,1)}, bf16[64,2048]{1,0:T(8,128)(2,1)S(1)}, u32[]{:S(2)}) copy-start(bf16[64,2048]{1,0:T(8,128)(2,1)S(1)} %get-tuple-element.17) | copy-start | bytes 786436
  602.1 51.5 %all-to-all-start.5 = ((bf16[128,16,256]{0,2,1:T(8,128)(2,1)}), bf16[128,16,256]{0,2,1:T(8,128)(2,1)S(1)}, u32[]{:S(2)}, u32[]{:S(2)}) async-start(bf16[128,16,256]{0,2,1:T(8,128)(2,1)} %bitcast.46), calls=%async_computation.6 | async-start | bytes 2097152 | tf_op jit(solution)/shard_map/all_to_all | solution.py:103
  653.6 40.2 %all-to-all-start.6 = ((bf16[128,16,256]{0,2,1:T(8,128)(2,1)}), bf16[128,16,256]{0,2,1:T(8,128)(2,1)S(1)}, u32[]{:S(2)}, u32[]{:S(2)}) async-start(bf16[128,16,256]{0,2,1:T(8,128)(2,1)} %bitcast.51), calls=%async_computation.7 | async-start | bytes 2097152 | tf_op jit(solution)/shard_map/all_to_all | solution.py:104
  662.1 101.7 %copy-start.10 = (bf16[16,16,8,256]{3,2,1,0:T(8,128)(2,1)S(1)}, bf16[16,16,8,256]{3,2,1,0:T(8,128)(2,1)}, u32[]{:S(2)}) copy-start(bf16[16,16,8,256]{3,2,1,0:T(8,128)(2,1)} %copy.84) | copy-start | bytes 3145732
  (12 other events, 175.4 us)
Sparse Core Ops, SparseCore 0:
  11.4 54.1 all-gather.13
  68.3 48.6 all-gather.11
  120.3 48.6 all-gather.17
  171.7 48.6 all-gather.19
  223.6 51.4 all-gather.15
  277.2 130.0 all-gather.9
  446.2 98.6 reduce-scatter.1
  547.6 52.1 all-gather.23
  602.6 48.6 all-gather.25
  653.5 110.1 all-gather.21
where the time goes:
time: 778 us; the launch traced here: 776 us
  waiting for transfers between devices  617 us (79%)
  local copies, waits for them, and re-layouts  50.1 us (6%)
  starting transfers between devices  48.4 us (6%)
  matrix products  23.2 us (3%)
  other arithmetic  21.8 us (3%)
  between operations  15.3 us (2%)
    reduce_scatter x1, waiting for transfers between devices, per_device(): lax.psum_scatter(lax.dot_general(gated, w_output, (((1,), (1,)), ((), ())...  96.5 us
    all_gather x1, waiting for transfers between devices, per_device(): lax.all_gather(normed_mid, 'mp', axis=0, tiled=True)  69.3 us
    all_gather x1, waiting for transfers between devices, per_device(): lax.all_gather(m_ffn_gate, 'dp', axis=0, tiled=True)  52.9 us
    all_gather x1, waiting for transfers between devices, per_device(): shard_piece = lax.all_gather(normed_in, 'mp', axis=0, tiled=True)  52.4 us
    all_gather x1, waiting for transfers between devices, per_device(): lax.all_gather(m_key, 'dp', axis=0, tiled=True)  52 us
    all_to_all x1, waiting for transfers between devices, per_device(): lax.all_to_all(r_value, 'mp', split_axis=1, concat_axis=0, tiled=True)  49 us
    all_gather x1, waiting for transfers between devices, per_device(): lax.all_gather(m_value, 'dp', axis=0, tiled=True)  45.4 us
    all_gather x1, waiting for transfers between devices, per_device(): lax.all_gather(m_swish, 'dp', axis=0, tiled=True)  42.8 us
  transfers between devices with their start and end apart: 17, of which 12 were waited for; matrix products, arithmetic and copies ran while one was open for 6% of the time, Pallas kernels for 0%

commit v1 on v0

v1 whole, which is shorter than its diff:
```python
import functools
import math

import jax
import jax.numpy as jnp
import numpy as np
from jax import lax
from jax.experimental import pallas as pl
from jax.experimental.pallas import tpu as pltpu
from jax.sharding import PartitionSpec as P

MESH = pl.DeviceIdType.MESH
F32, BF16 = jnp.float32, jnp.bfloat16
D, H, DK, DV = 2048, 8, 256, 512
SPAN, ROWS = 1024, 64
CA, CB = 2048, 1024
VMEM_LIMIT = 64 * 1024 * 1024 - 65536
ANY = pl.BlockSpec(memory_space=pl.ANY)
VM = pl.BlockSpec(memory_space=pltpu.VMEM)


class Spot:
    def __init__(self):
        dp, mp = lax.axis_index("dp"), lax.axis_index("mp")
        self.dp, self.mp = dp, mp
        self.y = lax.div(dp, 4)
        self.c = lax.rem(dp, 2)
        self.z = lax.div(mp, 2)
        self.xl = lax.rem(mp, 2)
        self.xh = lax.rem(lax.div(dp, 2), 2)
        self.x = self.xh * 2 + self.xl
        self.same = self.c == self.xl

    def at_z(self, step):
        z = lax.rem(self.z + (step + 8), 8)
        return z, (self.dp, z * 2 + self.xl)

    def sibling(self):
        return (self.dp + 1 - 2 * self.c, self.mp)

    def partner(self):
        return (self.dp + 1 - 2 * self.c, self.mp + 1 - 2 * self.xl)

    def across(self):
        return (self.dp, self.mp + 1 - 2 * self.xl)

    def plane(self, x, y):
        return (y * 4 + lax.div(x, 2) * 2 + self.c, self.z * 2 + lax.rem(x, 2))


def greet(peers):
    barrier = pltpu.get_barrier_semaphore()
    for peer in peers:
        pl.semaphore_signal(barrier, inc=1, device_id=peer, device_id_type=MESH)
    pl.semaphore_wait(barrier, len(peers))


class Post:
    def __init__(self, sends):
        self.sends, self.count, self.open = sends, 0, []

    def copy(self, src, dst, arrive, peer):
        return pltpu.make_async_remote_copy(
            src_ref=src, dst_ref=dst, send_sem=self.sends.at[self.count], recv_sem=arrive,
            device_id=peer, device_id_type=MESH,
        )

    def send(self, src, dst, arrive, peer):
        made = self.copy(src, dst, arrive, peer)
        self.count += 1
        made.start()
        self.open.append(made)

    def arrived(self, dst, arrive, peer):
        pltpu.make_async_remote_copy(
            src_ref=dst, dst_ref=dst, send_sem=self.sends.at[0], recv_sem=arrive,
            device_id=peer, device_id_type=MESH,
        ).wait_recv()

    def finish(self):
        for made in self.open:
            made.wait_send()


class PlaneGather:
    SENDS, FIRST, SECOND = 4 + 16 + 16, 4, 16

    def __init__(self, spot, post, w, first, second, sib):
        self.s, self.post, self.w = spot, post, w
        self.first, self.second, self.sib = first, second, sib
        c = spot.c
        u, v = (1 - c) * spot.x + c * spot.y, (1 - c) * spot.y + c * spot.x
        ring = lambda a, k: lax.rem(a + (k + 4), 4)
        order = (0, -1, 1, 2)
        self.us, self.vs = [ring(u, k) for k in order], [ring(v, k) for k in order]
        self.sus, self.svs = self.vs, self.us
        self.up, self.um = self.peer(ring(u, 1), v), self.peer(ring(u, -1), v)
        self.vp, self.vm = self.peer(u, ring(v, 1)), self.peer(u, ring(v, -1))

    def xy(self, u, v, c):
        return (1 - c) * u + c * v, (1 - c) * v + c * u

    def peer(self, u, v):
        return self.s.plane(*self.xy(u, v, self.s.c))

    def shard(self, u, v, c, half=None):
        x, y = self.xy(u, v, c)
        dp = y * 4 + lax.div(x, 2) * 2 + c
        rows = pl.ds(0, 8) if half is None else pl.ds(4 * half, 4)
        return self.w.at[dp, rows, lax.rem(x, 2)]

    def mine(self, r, t, half=None):
        return self.shard(self.us[r], self.vs[t], self.s.c, half)

    def neighbours(self):
        return [self.up, self.um, self.vp, self.vm, self.s.sibling()]

    def _go(self, ref, arrive, peer):
        self.post.send(ref, ref, arrive, peer)

    def own(self):
        ref = self.mine(0, 0)
        self._go(ref, self.first.at[0], self.up)
        self._go(ref, self.first.at[1], self.um)
        self._row(0)

    def _row(self, r):
        ref = self.mine(r, 0)
        self._go(ref, self.second.at[4 * r], self.vp)
        self._go(ref, self.second.at[4 * r + 1], self.vm)
        self._go(ref, self.sib.at[4 * r], self.s.sibling())

    def near_first(self):
        self.post.arrived(self.mine(1, 0), self.first.at[0], self.um)
        self._go(self.mine(1, 0, 0), self.first.at[2], self.up)
        self.post.arrived(self.mine(2, 0), self.first.at[1], self.up)
        self._go(self.mine(2, 0, 1), self.first.at[3], self.um)
        self._row(1)
        self._row(2)

    def far_first(self):
        self.post.arrived(self.mine(3, 0, 0), self.first.at[2], self.um)
        self.post.arrived(self.mine(3, 0, 1), self.first.at[3], self.up)
        self._row(3)

    def near_second(self, r):
        self.post.arrived(self.mine(r, 1), self.second.at[4 * r], self.vm)
        self._go(self.mine(r, 1, 0), self.second.at[4 * r + 2], self.vp)
        self.post.arrived(self.mine(r, 2), self.second.at[4 * r + 1], self.vp)
        self._go(self.mine(r, 2, 1), self.second.at[4 * r + 3], self.vm)
        self._go(self.mine(r, 1), self.sib.at[4 * r + 1], self.s.sibling())
        self._go(self.mine(r, 2), self.sib.at[4 * r + 2], self.s.sibling())

    def far_second(self, r):
        self.post.arrived(self.mine(r, 3, 0), self.second.at[4 * r + 2], self.vm)
        self.post.arrived(self.mine(r, 3, 1), self.second.at[4 * r + 3], self.vp)
        self._go(self.mine(r, 3), self.sib.at[4 * r + 3], self.s.sibling())

    def from_sibling(self):
        for r in range(4):
            for t in range(4):
                ref = self.shard(self.sus[r], self.svs[t], 1 - self.s.c)
                self.post.arrived(ref, self.sib.at[4 * r + t], self.s.sibling())


class RingGather:
    SENDS, ARRIVALS = 14, 16

    def __init__(self, spot, post, a, sems):
        self.s, self.post, self.a, self.sems = spot, post, a, sems

    def part(self, step, half):
        z, _ = self.s.at_z(step)
        return self.a.at[z, pl.ds(32 * half, 32)]

    def sem(self, way, step, half):
        return self.sems.at[way * 8 + step * 2 + half]

    def own(self, half, src=None):
        ref = self.part(0, half)
        for way, sign in ((0, 1), (1, -1)):
            self.post.send(ref if src is None else src, ref, self.sem(way, 0, half), self.s.at_z(sign)[1])

    def step(self, k, half):
        for way, sign in ((0, 1), (1, -1)):
            if k == 4 and half != way:
                continue
            ref = self.part(-sign * k, half)
            self.post.arrived(ref, self.sem(way, k - 1, half), self.s.at_z(-sign)[1])
            if k < 3 or (k == 3 and half == way):
                self.post.send(ref, ref, self.sem(way, k, half), self.s.at_z(sign)[1])


def local(src, dst, sem):
    made = pltpu.make_async_copy(src, dst, sem)
    made.start()
    return made


def prep_kernel(tok, gain, decay, length, q, k, v, g, o, fg, fu, nrm, wa, wb, small):
    z = lax.div(lax.axis_index("mp"), 2)
    values = tok[...].astype(F32)
    scale = lax.rsqrt(jnp.mean(values * values, axis=-1, keepdims=True) + 1e-06)
    nrm[...] = (values * scale * gain[...]).astype(BF16)
    for h in range(H):
        wa[h, :, 0:256] = q[:, h * 256 : h * 256 + 256].astype(BF16)
        wa[h, :, 256:512] = k[:, h * 256 : h * 256 + 256].astype(BF16)
        wa[h, :, 512:1024] = v[:, h * 512 : h * 512 + 512].astype(BF16)
        wa[h, :, 1024:1536] = g[:, h * 512 : h * 512 + 512].astype(BF16)
        wa[h, :, 1536:2048] = o[:, h * 512 : h * 512 + 512].astype(BF16)
        wb[h, :, 0:512] = fg[:, h * 512 : h * 512 + 512].astype(BF16)
        wb[h, :, 512:1024] = fu[:, h * 512 : h * 512 + 512].astype(BF16)
    total = decay[...]
    lane = lax.broadcasted_iota(jnp.int32, (H, SPAN), 1)
    reach = 1
    while reach < SPAN:
        total = total + jnp.where(lane >= reach, pltpu.roll(total, reach, 1), 0.0)
        reach *= 2
    row = lax.broadcasted_iota(jnp.int32, (H, SPAN), 0)
    chosen = jnp.sum(jnp.where(row == z, total, 0.0), axis=0, keepdims=True)
    small[...] = jnp.where(row < 4, chosen, length[0, 0])


def prep(*args):
    return pl.pallas_call(
        prep_kernel,
        out_shape=(
            jax.ShapeDtypeStruct((ROWS, D), BF16),
            jax.ShapeDtypeStruct((8, 8, CA), BF16),
            jax.ShapeDtypeStruct((8, 8, CB), BF16),
            jax.ShapeDtypeStruct((8, SPAN), F32),
        ),
        in_specs=[VM] * 3 + [pl.BlockSpec(memory_space=pltpu.SMEM)] + [VM] * 7,
        out_specs=(VM,) * 4,
        name="prep",
    )(*args)


def gather_kernel(nrm, tok, wa, small, acts, tokw, smallw, w, sends, zr, az, p1, p2, ps, misc, lsem):
    s = Spot()
    post = Post(sends)
    plane = PlaneGather(s, post, w, p1, p2, ps)
    greet([s.at_z(k)[1] for k in range(1, 8)] + plane.neighbours() + [s.partner()])

    own = local(wa.at[s.z], w.at[s.dp, s.z, s.xl], lsem.at[0])
    for k in range(1, 8):
        zd, peer = s.at_z(k)
        post.send(wa.at[zd], w.at[s.dp, s.z, s.xl], az.at[k], peer)
    def trade(src, dst, which):
        return pltpu.make_async_remote_copy(
            src_ref=src, dst_ref=dst, send_sem=lsem.at[which], recv_sem=misc.at[which],
            device_id=s.partner(), device_id_type=MESH,
        )

    @pl.when(s.same)
    def _():
        local(nrm, acts.at[s.z], lsem.at[1])
        local(tok, tokw, lsem.at[2])

    @pl.when(jnp.logical_not(s.same))
    def _():
        trade(nrm, acts.at[s.z], 1).start()
        trade(tok, tokw, 2).start()

    post.send(small, smallw, misc.at[0], s.sibling())

    @pl.when(s.same)
    def _():
        pltpu.make_async_copy(nrm, acts.at[s.z], lsem.at[1]).wait()

    @pl.when(jnp.logical_not(s.same))
    def _():
        trade(nrm, acts.at[s.z], 1).wait_recv()

    own.wait()
    for k in range(1, 8):
        zs, peer = s.at_z(-k)
        post.arrived(w.at[s.dp, zs, s.xl], az.at[k], peer)

    ring = RingGather(s, post, acts, zr)
    plane.own()
    ring.own(0)
    ring.own(1)
    plane.near_first()
    ring.step(1, 0)
    ring.step(1, 1)
    plane.far_first()
    plane.near_second(0)
    ring.step(2, 0)
    plane.near_second(1)
    ring.step(2, 1)
    plane.near_second(2)
    plane.far_second(0)
    ring.step(3, 0)
    ring.step(3, 1)
    plane.near_second(3)
    plane.far_second(1)
    plane.far_second(2)
    plane.far_second(3)
    ring.step(4, 0)
    ring.step(4, 1)
    plane.from_sibling()
    post.arrived(smallw, misc.at[0], s.sibling())

    @pl.when(s.same)
    def _():
        pltpu.make_async_copy(tok, tokw, lsem.at[2]).wait()

    @pl.when(jnp.logical_not(s.same))
    def _():
        trade(nrm, acts.at[s.z], 1).wait_send()
        trade(tok, tokw, 2).wait()

    post.finish()


def gather(nrm, tok, wa, small):
    return pl.pallas_call(
        gather_kernel,
        out_shape=(
            jax.ShapeDtypeStruct((8, ROWS, D), BF16),
            jax.ShapeDtypeStruct((ROWS, D), BF16),
            jax.ShapeDtypeStruct((8, SPAN), F32),
            jax.ShapeDtypeStruct((16, 8, 2, 8, CA), BF16),
        ),
        in_specs=[VM] * 4,
        out_specs=(ANY,) * 4,
        scratch_shapes=[
            pltpu.SemaphoreType.DMA((7 + 1 + PlaneGather.SENDS + RingGather.SENDS,)),
            pltpu.SemaphoreType.DMA((16,)),
            pltpu.SemaphoreType.DMA((8,)),
            pltpu.SemaphoreType.DMA((4,)),
            pltpu.SemaphoreType.DMA((16,)),
            pltpu.SemaphoreType.DMA((16,)),
            pltpu.SemaphoreType.DMA((3,)),
            pltpu.SemaphoreType.DMA((4,)),
        ],
        compiler_params=pltpu.CompilerParams(collective_id=0, has_side_effects=True, vmem_limit_bytes=VMEM_LIMIT),
        name="gather",
    )(nrm, tok, wa, small)


def turn_tables():
    frequency = 10000.0 ** (-(np.arange(DK) // 2 * 2) / DK)
    sign = np.where(np.arange(DK) % 2 == 0, -1.0, 1.0)
    far = (np.arange(8) * 128.0)[:, None] * frequency[None]
    near = np.arange(128.0)[:, None] * frequency[None]
    table_far = np.stack([np.cos(far), np.sin(far)]).astype(np.float32)
    table_near = np.stack([np.cos(near), np.sin(near)]).astype(np.float32)
    return table_far, table_near, sign.astype(np.float32)[None]


def head_kernel(
    acts, w, small, smallw, far, near, sign, wb, part, wbp,
    kv, cosine, sine, qs, gs, column, gated, sends, az, misc,
):
    s = Spot()
    post = Post(sends)
    greet([s.at_z(k)[1] for k in range(1, 8)] + [s.sibling()])
    own = local(wb.at[s.z], wbp.at[s.dp, s.z, s.xl], misc.at[0])
    for k in range(1, 8):
        zd, peer = s.at_z(k)
        post.send(wb.at[zd], wbp.at[s.dp, s.z, s.xl], az.at[k], peer)

    base = pl.multiple_of(64 * s.c, 64)
    cn, sn = near[0, pl.ds(base, 64)], near[1, pl.ds(base, 64)]
    for b in range(8):
        cf, sf = far[0, b : b + 1], far[1, b : b + 1]
        cosine[b] = cf * cn - sf * sn
        sine[b] = (sf * cn + cf * sn) * sign[...]
    even = lax.rem(lax.broadcasted_iota(jnp.int32, (256, DK), 1), 2) == 0

    def rot(u, tile):
        c4 = cosine[pl.ds(4 * tile, 4)].reshape(256, DK)
        s4 = sine[pl.ds(4 * tile, 4)].reshape(256, DK)
        swapped = jnp.where(even, pltpu.roll(u, DK - 1, 1), pltpu.roll(u, 1, 1))
        return u * c4 + swapped * s4

    def project(tile, low, width):
        rows = acts[pl.ds(4 * tile, 4)].reshape(256, D)
        return jnp.dot(rows, w[:, low : low + width], preferred_element_type=F32)

    for tile in range(2):
        turned = rot(project(tile, 256, 256), tile).astype(BF16)
        kv[pl.ds(4 * tile, 4), s.c, :, 0:256] = turned.reshape(4, 64, 256)
        values = project(tile, 512, 512).astype(BF16)
        kv[pl.ds(4 * tile, 4), s.c, :, 256:768] = values.reshape(4, 64, 512)
    post.send(kv.at[:, s.c], kv.at[:, s.c], misc.at[1], s.sibling())
    for tile in range(2):
        qs[pl.ds(256 * tile, 256)] = rot(project(tile, 0, 256), tile).astype(BF16)
        gs[pl.ds(256 * tile, 256)] = project(tile, 1024, 512).astype(BF16)
    chosen = jnp.where(s.same, small[...], smallw[...])
    run_row = chosen[0:1]
    length = chosen[4:5, 0:1]
    column[...] = jnp.broadcast_to(run_row, (128, SPAN)).T
    post.arrived(kv.at[:, 1 - s.c], misc.at[1], s.sibling())

    for tile in range(4):
        keys = 256 * (tile + 1)
        q = qs[pl.ds(128 * tile, 128)]
        k = kv[pl.ds(0, 2 * (tile + 1)), :, :, 0:256].reshape(keys, 256)
        v = kv[pl.ds(0, 2 * (tile + 1)), :, :, 256:768].reshape(keys, 512)
        scores = lax.dot_general(q, k, (((1,), (1,)), ((), ())), preferred_element_type=F32) * (DK**-0.5)
        local_row = lax.broadcasted_iota(jnp.int32, (128, 1), 0)
        place = 256 * tile + local_row + jnp.where(local_row >= 64, 64, 0) + 64 * s.c
        at = lax.broadcasted_iota(jnp.int32, (128, keys), 1)
        low = pl.multiple_of(256 * tile + 64 * s.c, 64)
        run_col = jnp.concatenate([column[pl.ds(low, 64), 0:1], column[pl.ds(low + 128, 64), 0:1]], axis=0)
        gap = run_col - run_row[:, :keys]
        weights = (scores * jnp.exp(jnp.where(place >= at, gap, -jnp.inf))).astype(BF16)
        kept = jnp.dot(weights, v, preferred_element_type=F32)
        mean = jnp.mean(kept, axis=-1, keepdims=True)
        spread = jnp.mean(kept * kept, axis=-1, keepdims=True) - mean * mean
        normed = (kept - mean) * lax.rsqrt(spread + 1e-05)
        gate = gs[pl.ds(128 * tile, 128)].astype(F32)
        out = gate / (1.0 + jnp.exp(-gate)) * normed
        live = place.astype(F32) < length
        gated[pl.ds(128 * tile, 128)] = jnp.where(live, out, 0.0).astype(BF16)

    for tile in range(4):
        cols = pl.ds(512 * tile, 512)
        wo = w[cols, 1536:2048]
        out = lax.dot_general(gated[...], wo, (((1,), (1,)), ((), ())), preferred_element_type=F32)
        part[:, :, cols] = out.astype(BF16).reshape(8, 64, 512)

    own.wait()
    for k in range(1, 8):
        zs, peer = s.at_z(-k)
        post.arrived(wbp.at[s.dp, zs, s.xl], az.at[k], peer)
    post.finish()


def head(acts, w, small, smallw, wb):
    far, near, sign = turn_tables()
    return pl.pallas_call(
        head_kernel,
        out_shape=(
            jax.ShapeDtypeStruct((8, ROWS, D), BF16),
            jax.ShapeDtypeStruct((16, 8, 2, 8, CB), BF16),
        ),
        in_specs=[VM] * 8,
        out_specs=(VM, ANY),
        scratch_shapes=[
            pltpu.VMEM((8, 2, ROWS, 768), BF16),
            pltpu.VMEM((8, ROWS, DK), F32),
            pltpu.VMEM((8, ROWS, DK), F32),
            pltpu.VMEM((512, DK), BF16),
            pltpu.VMEM((512, DV), BF16),
            pltpu.VMEM((SPAN, 128), F32),
            pltpu.VMEM((512, DV), BF16),
            pltpu.SemaphoreType.DMA((8,)),
            pltpu.SemaphoreType.DMA((8,)),
            pltpu.SemaphoreType.DMA((2,)),
        ],
        compiler_params=pltpu.CompilerParams(collective_id=1, has_side_effects=True, vmem_limit_bytes=VMEM_LIMIT),
        name="head",
    )(acts, w.reshape(D, CA), small, smallw, far, near, sign, wb)


def middle_kernel(
    part, tokw, gain, wb_in, acts, res, w,
    got, out_box, nbuf, rbuf, sends, rr, zr, p1, p2, ps, misc,
):
    s = Spot()
    post = Post(sends)
    plane = PlaneGather(s, post, w, p1, p2, ps)
    greet([s.at_z(1)[1], s.at_z(-1)[1]] + plane.neighbours() + [s.partner()])

    ways = ((0, 1), (1, -1))

    def rs_send(way, sign, hop, half, src):
        post.send(
            src, got.at[way, hop, pl.ds(32 * half, 32)], rr.at[way * 8 + hop * 2 + half], s.at_z(sign)[1]
        )

    def rs_wait(way, sign, hop, half):
        post.arrived(
            got.at[way, hop, pl.ds(32 * half, 32)], rr.at[way * 8 + hop * 2 + half], s.at_z(-sign)[1]
        )

    def rows(half):
        return pl.ds(32 * half, 32)

    for way, sign in ways:
        rs_send(way, sign, 0, way, part.at[s.at_z(4 * sign)[0], rows(way)])
        rs_send(way, sign, 1, 1 - way, part.at[s.at_z(3 * sign)[0], rows(1 - way)])
    plane.own()

    def relay(hop, half):
        for way, sign in ways:
            if hop == 1 and half != way:
                continue
            rs_wait(way, sign, hop - 1, half)
            here = part[s.at_z((4 - hop) * sign)[0], rows(half)].astype(F32)
            both = here + got[way, hop - 1, rows(half)].astype(F32)
            out_box[way, hop - 1, rows(half)] = both.astype(BF16)
            rs_send(way, sign, hop, half, out_box.at[way, hop - 1, rows(half)])

    relay(1, 0)
    relay(1, 1)
    plane.near_first()
    relay(2, 1)
    relay(2, 0)
    plane.far_first()
    plane.near_second(0)
    relay(3, 1)
    relay(3, 0)
    plane.near_second(1)
    plane.near_second(2)
    plane.far_second(0)

    ring = RingGather(s, post, acts, zr)
    for half in (1, 0):
        for way, sign in ways:
            rs_wait(way, sign, 3, half)
        branch = (
            part[s.z, rows(half)].astype(F32)
            + got[0, 3, rows(half)].astype(F32)
            + got[1, 3, rows(half)].astype(F32)
        )
        residual = (tokw[rows(half)].astype(F32) + branch).astype(BF16)
        rbuf[rows(half)] = residual
        values = residual.astype(F32)
        scale = lax.rsqrt(jnp.mean(values * values, axis=-1, keepdims=True) + 1e-06)
        nbuf[rows(half)] = (values * scale * gain[...]).astype(BF16)
        local(nbuf.at[rows(half)], acts.at[s.z, rows(half)], misc.at[half])
        ring.own(half, nbuf.at[rows(half)])

    slot = post.count
    post.count += 1

    def hand_back():
        return pltpu.make_async_remote_copy(
            src_ref=rbuf, dst_ref=res, send_sem=sends.at[slot], recv_sem=misc.at[2],
            device_id=s.partner(), device_id_type=MESH,
        )

    @pl.when(s.same)
    def _():
        local(rbuf, res, misc.at[3])

    @pl.when(jnp.logical_not(s.same))
    def _():
        hand_back().start()

    plane.near_second(3)
    plane.far_second(1)
    plane.far_second(2)
    ring.step(1, 1)
    ring.step(1, 0)
    plane.far_second(3)
    ring.step(2, 1)
    ring.step(2, 0)
    plane.from_sibling()
    ring.step(3, 1)
    ring.step(3, 0)
    ring.step(4, 1)
    ring.step(4, 0)

    @pl.when(s.same)
    def _():
        pltpu.make_async_copy(rbuf, res, misc.at[3]).wait()

    @pl.when(jnp.logical_not(s.same))
    def _():
        hand_back().wait()

    for half in range(2):
        pltpu.make_async_copy(nbuf.at[rows(half)], acts.at[s.z, rows(half)], misc.at[half]).wait()
    post.finish()


def middle(part, tokw, gain, wb):
    return pl.pallas_call(
        middle_kernel,
        out_shape=(
            jax.ShapeDtypeStruct((8, ROWS, D), BF16),
            jax.ShapeDtypeStruct((ROWS, D), BF16),
            jax.ShapeDtypeStruct((16, 8, 2, 8, CB), BF16),
        ),
        in_specs=[VM] * 3 + [ANY],
        out_specs=(ANY,) * 3,
        input_output_aliases={3: 2},
        scratch_shapes=[
            pltpu.VMEM((2, 4, ROWS, D), BF16),
            pltpu.VMEM((2, 3, ROWS, D), BF16),
            pltpu.VMEM((ROWS, D), BF16),
            pltpu.VMEM((ROWS, D), BF16),
            pltpu.SemaphoreType.DMA((14 + 1 + PlaneGather.SENDS + RingGather.SENDS,)),
            pltpu.SemaphoreType.DMA((16,)),
            pltpu.SemaphoreType.DMA((16,)),
            pltpu.SemaphoreType.DMA((4,)),
            pltpu.SemaphoreType.DMA((16,)),
            pltpu.SemaphoreType.DMA((16,)),
            pltpu.SemaphoreType.DMA((4,)),
        ],
        compiler_params=pltpu.CompilerParams(collective_id=2, has_side_effects=True, vmem_limit_bytes=VMEM_LIMIT),
        name="middle",
    )(part, tokw, gain, wb)


def hidden_kernel(acts, w, out, box, sends, misc):
    s = Spot()
    post = Post(sends)
    greet([s.sibling(), s.across(), s.partner()])

    def half(j, slot):
        for tile in range(2):
            rows = acts[pl.ds(4 * tile, 4)].reshape(256, D)
            low = pl.multiple_of(256 * j, 256)
            gate = jnp.dot(rows, w[:, pl.ds(low, 256)], preferred_element_type=F32)
            up = jnp.dot(rows, w[:, pl.ds(pl.multiple_of(low + 512, 256), 256)], preferred_element_type=F32)
            made = (gate / (1.0 + jnp.exp(-gate)) * up).astype(BF16)
            box[slot, pl.ds(4 * tile, 4)] = made.reshape(4, 64, 256)

    def give(slot, peer, arrive):
        return pltpu.make_async_remote_copy(
            src_ref=box.at[slot], dst_ref=out.at[:, s.c], send_sem=sends.at[slot], recv_sem=misc.at[arrive],
            device_id=peer, device_id_type=MESH,
        )

    half(1 - s.xl, 0)

    @pl.when(s.same)
    def _():
        give(0, s.across(), 0).start()

    @pl.when(jnp.logical_not(s.same))
    def _():
        give(0, s.partner(), 2).start()

    half(s.xl, 1)

    @pl.when(s.same)
    def _():
        kept = local(box.at[1], out.at[:, s.c], misc.at[3])
        kept.wait()
        post.arrived(out.at[:, 1 - s.c], misc.at[1], s.sibling())
        give(0, s.across(), 0).wait_send()

    @pl.when(jnp.logical_not(s.same))
    def _():
        give(1, s.sibling(), 1).start()
        post.arrived(out.at[:, s.c], misc.at[0], s.across())
        post.arrived(out.at[:, 1 - s.c], misc.at[2], s.partner())
        give(0, s.partner(), 2).wait_send()
        give(1, s.sibling(), 1).wait_send()


def hidden(acts, w):
    made = pl.pallas_call(
        hidden_kernel,
        out_shape=jax.ShapeDtypeStruct((8, 2, ROWS, 256), BF16),
        in_specs=[VM] * 2,
        out_specs=ANY,
        scratch_shapes=[
            pltpu.VMEM((2, 8, ROWS, 256), BF16),
            pltpu.SemaphoreType.DMA((2,)),
            pltpu.SemaphoreType.DMA((4,)),
        ],
        compiler_params=pltpu.CompilerParams(collective_id=3, has_side_effects=True, vmem_limit_bytes=VMEM_LIMIT),
        name="hidden",
    )(acts, w.reshape(D, CB))
    return made.reshape(SPAN, 256)


def per_device(tokens, norm_gain, mlp_gain, lengths, log_decay, q, k, v, g, o, fg, fu):
    nrm, wa, wb, small = prep(
        tokens, norm_gain.reshape(1, D), log_decay.T, lengths.astype(F32).reshape(1, 1), q, k, v, g, o.T, fg, fu
    )
    acts, tokw, smallw, w = gather(nrm, tokens, wa, small)
    part, wb = head(acts, w, small, smallw, wb)
    acts, residual, wb = middle(part, tokw, mlp_gain.reshape(1, D), wb)
    return residual, hidden(acts, wb)


def solution(mesh):
    rows = P(("dp", "mp"), None)
    placed = (rows, P(), P(), P("dp"), P("dp", None), rows, rows, rows, rows, P(None, ("dp", "mp")), rows, rows)
    return jax.shard_map(
        per_device, mesh=mesh, in_specs=placed, out_specs=(rows, P("dp", "mp")), check_vma=False
    )
```

time: 778 us -> 134 us (0.17)
  waiting for transfers between devices: 617 us -> 0 us
  Pallas kernels: 0 us -> 129 us
  starting transfers between devices: 48.4 us -> 0 us
  local copies, waits for them, and re-layouts: 50.1 us -> 3.54 us
  matrix products: 23.2 us -> 0 us
  other arithmetic: 21.8 us -> 0 us
  between operations: 15.3 us -> 1.31 us
    all_gather x9 -> x0, waiting for transfers between devices: 440 us -> none  [the longest x1 69.3 us: per_device(): lax.all_gather(normed_mid, 'mp', axis=0, tiled=True)]
    pallas_call x0 -> x5, Pallas kernels: none -> 129 us  [the longest x1 48.2 us: gather(): pl.pallas_call(gather_kernel, out_shape=(jax.ShapeDtypeStruct((8, ROWS, D...]
    reduce_scatter x1 -> x0, waiting for transfers between devices: 96.5 us -> none  [per_device(): lax.psum_scatter(lax.dot_general(gated, w_output, (((1,), (1,)), ((), ())...]
    all_to_all x7 -> x0, waiting for transfers between devices: 80.7 us -> none  [the longest x1 49 us: per_device(): lax.all_to_all(r_value, 'mp', split_axis=1, concat_axis=0, tiled=True)]
    all_to_all x7 -> x0, starting transfers between devices: 48 us -> none  [the longest x1 6.91 us: per_device(): lax.all_to_all(r_output, 'mp', split_axis=1, concat_axis=0, tiled=True)]
    dot_general x5 -> x0, matrix products: 23.2 us -> none  [the longest x1 9.87 us: per_device(): jnp.dot(shard_piece, merged_weights, preferred_element_type=jnp.float32)]
    all_gather x7 -> x0, local copies, waits for them, and re-layouts: 17.7 us -> none  [the longest x1 4.1 us: per_device(): lax.all_gather(m_value, 'dp', axis=0, tiled=True)]
    transpose x7 -> x0, local copies, waits for them, and re-layouts: 11.3 us -> none  [trainer_order(): return split_rows.transpose(1, 0, 2, 3).reshape(row_total, columns)]
  transfers between devices with their start and end apart: 17 -> 0, of which waited for: 12 -> 0; matrix products, arithmetic and copies ran while one was open for 6% -> 0% of each run, Pallas kernels for 0% -> 0%
where the time goes in v1:
time: 134 us
  Pallas kernels  129 us (96%)
  local copies, waits for them, and re-layouts  3.54 us (3%)
    pallas_call x1, Pallas kernels, gather(): pl.pallas_call(gather_kernel, out_shape=(jax.ShapeDtypeStruct((8, ROWS, D...  48.2 us
    pallas_call x1, Pallas kernels, middle(): pl.pallas_call(middle_kernel, out_shape=(jax.ShapeDtypeStruct((8, ROWS, D...  48.1 us
    pallas_call x1, Pallas kernels, head(): pl.pallas_call(head_kernel, out_shape=(jax.ShapeDtypeStruct((8, ROWS, D),...  15.1 us
    pallas_call x1, Pallas kernels, hidden(): pl.pallas_call(hidden_kernel, out_shape=jax.ShapeDtypeStruct((8, 2, ROWS,...  15.1 us
    unnamed x2, local copies, waits for them, and re-layouts  3.54 us

profile of v1, /device:TPU:1, one launch (start us, length us, event | category | flops | bytes accessed | tf_op | source)
XLA Modules:
  0.0 134.0 jit_solution(6048473041026182161)
XLA Ops:
  1.3 2.6 %prep.1 = (bf16[64,2048]{1,0:T(8,128)(2,1)}, bf16[8,8,2048]{2,1,0:T(8,128)(2,1)}, bf16[8,8,1024]{2,1,0:T(8,128)(2,1)}, f32[8,1024]{1,0:T(8,128)}) custom-call(bf16[64,2048]{1,0:T(8,128)(2,1)} %tok.3, f32[1,2048]{1,0:T(1,128)} %bitcast.13, f32[8,1024]{1,0:T(8,128)} %bitcast.12, f32[1,1]{1,0:T(1,128)} %bitcast.2.length, f32[8,2048]{1,0:T(8,128)} %q.1, ...), custom_call_target="tpu_custom_call" | custom-call | tf_op jit(solution)/shard_map/prep/pallas_call | solution.py:225
  3.9 48.2 %gather.1 = (bf16[8,64,2048]{2,1,0:T(8,128)(2,1)}, bf16[64,2048]{1,0:T(8,128)(2,1)}, f32[8,1024]{1,0:T(8,128)}, bf16[16,8,2,8,2048]{4,3,2,1,0:T(8,128)(2,1)}) custom-call(bf16[64,2048]{1,0:T(8,128)(2,1)} %get-tuple-element.15.nrm, bf16[64,2048]{1,0:T(8,128)(2,1)} %tok.3, bf16[8,8,2048]{2,1,0:T(8,128)(2,1)} %get-tuple-element.16.wa, ...), custom_call_target="tpu_custom_call" | custom-call | tf_op jit(solution)/shard_map/gather/pallas_call | solution.py:318
  52.1 15.1 %head.1 = (bf16[8,64,2048]{2,1,0:T(8,128)(2,1)}, bf16[16,8,2,8,1024]{4,3,2,1,0:T(8,128)(2,1)}) custom-call(bf16[8,64,2048]{2,1,0:T(8,128)(2,1)} %get-tuple-element.18.acts, bf16[2048,2048]{1,0:T(8,128)(2,1)} %bitcast.9, f32[8,1024]{1,0:T(8,128)} %get-tuple-element.17.small, f32[8,1024]{1,0:T(8,128)} %get-tuple-element.20.smallw, ...), custom_call_target="tpu_custom_call" | custom-call | tf_op jit(solution)/shard_map/head/pallas_call | solution.py:435
  67.3 48.1 %middle.1 = (bf16[8,64,2048]{2,1,0:T(8,128)(2,1)}, bf16[64,2048]{1,0:T(8,128)(2,1)}, bf16[16,8,2,8,1024]{4,3,2,1,0:T(8,128)(2,1)}) custom-call(bf16[8,64,2048]{2,1,0:T(8,128)(2,1)} %get-tuple-element.22.part, bf16[64,2048]{1,0:T(8,128)(2,1)} %get-tuple-element.23.tokw, f32[1,2048]{1,0:T(1,128)} %bitcast.14, ...), custom_call_target="tpu_custom_call", output_to_operand_aliasing={{2}: (3, {})} | custom-call | tf_op jit(solution)/shard_map/middle/pallas_call | solution.py:574
  115.4 15.1 %hidden.1 = bf16[8,2,64,256]{3,2,1,0:T(8,128)(2,1)} custom-call(bf16[8,64,2048]{2,1,0:T(8,128)(2,1)} %get-tuple-element.26.acts, bf16[2048,1024]{1,0:T(8,128)(2,1)} %bitcast.8), custom_call_target="tpu_custom_call" | custom-call | tf_op jit(solution)/shard_map/hidden/pallas_call | solution.py:651
  130.5 1.7 %copy.22 = bf16[64,2048]{1,0:T(8,128)(2,1)} copy(bf16[64,2048]{1,0:T(8,128)(2,1)} %get-tuple-element.30) | data formatting | bytes 524288
  132.2 1.9 %copy.23 = bf16[1024,256]{1,0:T(8,128)(2,1)} copy(bf16[1024,256]{1,0:T(8,128)(2,1)} %bitcast.10) | data formatting | bytes 1048576

commit v2 on v1

v2 whole, which is shorter than its diff:
```python
import functools
import math

import jax
import jax.numpy as jnp
import numpy as np
from jax import lax
from jax.experimental import pallas as pl
from jax.experimental.pallas import tpu as pltpu
from jax.sharding import PartitionSpec as P

MESH = pl.DeviceIdType.MESH
F32, BF16 = jnp.float32, jnp.bfloat16
D, H, DK, DV = 2048, 8, 256, 512
SPAN, ROWS = 1024, 64
CA, CB = 2048, 1024
VMEM_LIMIT = 64 * 1024 * 1024 - 65536
ANY = pl.BlockSpec(memory_space=pl.ANY)
SM = pl.BlockSpec(memory_space=pltpu.SMEM)
VM = pl.BlockSpec(memory_space=pltpu.VMEM)


class Spot:
    def __init__(self):
        dp, mp = lax.axis_index("dp"), lax.axis_index("mp")
        self.dp, self.mp = dp, mp
        self.y = lax.div(dp, 4)
        self.c = lax.rem(dp, 2)
        self.z = lax.div(mp, 2)
        self.xl = lax.rem(mp, 2)
        self.xh = lax.rem(lax.div(dp, 2), 2)
        self.x = self.xh * 2 + self.xl
        self.same = self.c == self.xl

    def at_z(self, step):
        z = lax.rem(self.z + (step + 8), 8)
        return z, (self.dp, z * 2 + self.xl)

    def sibling(self):
        return (self.dp + 1 - 2 * self.c, self.mp)

    def partner(self):
        return (self.dp + 1 - 2 * self.c, self.mp + 1 - 2 * self.xl)

    def across(self):
        return (self.dp, self.mp + 1 - 2 * self.xl)

    def plane(self, x, y):
        return (y * 4 + lax.div(x, 2) * 2 + self.c, self.z * 2 + lax.rem(x, 2))


class Post:
    def __init__(self, sends):
        self.sends, self.count, self.open = sends, 0, []

    def copy(self, src, dst, arrive, peer):
        return pltpu.make_async_remote_copy(
            src_ref=src, dst_ref=dst, send_sem=self.sends.at[self.count], recv_sem=arrive,
            device_id=peer, device_id_type=MESH,
        )

    def send(self, src, dst, arrive, peer):
        made = self.copy(src, dst, arrive, peer)
        self.count += 1
        made.start()
        self.open.append(made)

    def arrived(self, dst, arrive, peer):
        pltpu.make_async_remote_copy(
            src_ref=dst, dst_ref=dst, send_sem=self.sends.at[0], recv_sem=arrive,
            device_id=peer, device_id_type=MESH,
        ).wait_recv()

    def finish(self):
        for made in self.open:
            made.wait_send()


class PlaneGather:
    SENDS, FIRST, SECOND = 4 + 16 + 16, 4, 16

    def __init__(self, spot, post, w, cols, first, second, sib):
        self.s, self.post, self.w, self.cols = spot, post, w, cols
        self.first, self.second, self.sib = first, second, sib
        c = spot.c
        u, v = (1 - c) * spot.x + c * spot.y, (1 - c) * spot.y + c * spot.x
        ring = lambda a, k: lax.rem(a + (k + 4), 4)
        order = (0, -1, 1, 2)
        self.us, self.vs = [ring(u, k) for k in order], [ring(v, k) for k in order]
        self.sus, self.svs = self.vs, self.us
        self.up, self.um = self.peer(ring(u, 1), v), self.peer(ring(u, -1), v)
        self.vp, self.vm = self.peer(u, ring(v, 1)), self.peer(u, ring(v, -1))

    def xy(self, u, v, c):
        return (1 - c) * u + c * v, (1 - c) * v + c * u

    def peer(self, u, v):
        return self.s.plane(*self.xy(u, v, self.s.c))

    def shard(self, u, v, c, half=None):
        x, y = self.xy(u, v, c)
        dp = y * 4 + lax.div(x, 2) * 2 + c
        rows = pl.ds(0, 8) if half is None else pl.ds(4 * half, 4)
        return self.w.at[dp, rows, lax.rem(x, 2), :, self.cols]

    def mine(self, r, t, half=None):
        return self.shard(self.us[r], self.vs[t], self.s.c, half)

    def neighbours(self):
        return [self.up, self.um, self.vp, self.vm, self.s.sibling()]

    def _go(self, ref, arrive, peer):
        self.post.send(ref, ref, arrive, peer)

    def own(self):
        ref = self.mine(0, 0)
        self._go(ref, self.first.at[0], self.up)
        self._go(ref, self.first.at[1], self.um)
        self._row(0)

    def _row(self, r):
        ref = self.mine(r, 0)
        self._go(ref, self.second.at[4 * r], self.vp)
        self._go(ref, self.second.at[4 * r + 1], self.vm)
        self._go(ref, self.sib.at[4 * r], self.s.sibling())

    def near_first(self):
        self.post.arrived(self.mine(1, 0), self.first.at[0], self.um)
        self._go(self.mine(1, 0, 0), self.first.at[2], self.up)
        self.post.arrived(self.mine(2, 0), self.first.at[1], self.up)
        self._go(self.mine(2, 0, 1), self.first.at[3], self.um)
        self._row(1)
        self._row(2)

    def far_first(self):
        self.post.arrived(self.mine(3, 0, 0), self.first.at[2], self.um)
        self.post.arrived(self.mine(3, 0, 1), self.first.at[3], self.up)
        self._row(3)

    def near_second(self, r):
        self.post.arrived(self.mine(r, 1), self.second.at[4 * r], self.vm)
        self._go(self.mine(r, 1, 0), self.second.at[4 * r + 2], self.vp)
        self.post.arrived(self.mine(r, 2), self.second.at[4 * r + 1], self.vp)
        self._go(self.mine(r, 2, 1), self.second.at[4 * r + 3], self.vm)
        self._go(self.mine(r, 1), self.sib.at[4 * r + 1], self.s.sibling())
        self._go(self.mine(r, 2), self.sib.at[4 * r + 2], self.s.sibling())

    def far_second(self, r):
        self.post.arrived(self.mine(r, 3, 0), self.second.at[4 * r + 2], self.vm)
        self.post.arrived(self.mine(r, 3, 1), self.second.at[4 * r + 3], self.vp)
        self._go(self.mine(r, 3), self.sib.at[4 * r + 3], self.s.sibling())

    def from_sibling(self):
        for r in range(4):
            for t in range(4):
                ref = self.shard(self.sus[r], self.svs[t], 1 - self.s.c)
                self.post.arrived(ref, self.sib.at[4 * r + t], self.s.sibling())


def slot_of(r):
    return (r + 2) % 8


NEAR, FAR = (0, 5), (5, 3)


class RingGather:
    SENDS, ARRIVALS = 14, 16

    def __init__(self, spot, post, a, sems):
        self.s, self.post, self.a, self.sems = spot, post, a, sems

    def part(self, r, half):
        return self.a.at[slot_of(r), pl.ds(32 * half, 32)]

    def sem(self, way, step, half):
        return self.sems.at[way * 8 + step * 2 + half]

    def own(self, half):
        for way, sign in ((0, 1), (1, -1)):
            self.post.send(self.part(0, half), self.part(-sign, half), self.sem(way, 0, half), self.s.at_z(sign)[1])

    def step(self, k, half):
        for way, sign in ((0, 1), (1, -1)):
            if k == 4 and half != way:
                continue
            ref = self.part(-sign * k, half)
            self.post.arrived(ref, self.sem(way, k - 1, half), self.s.at_z(-sign)[1])
            if k < 3 or (k == 3 and half == way):
                self.post.send(ref, self.part(-sign * (k + 1), half), self.sem(way, k, half), self.s.at_z(sign)[1])


def local(src, dst, sem):
    made = pltpu.make_async_copy(src, dst, sem)
    made.start()
    return made


def turn_tables():
    frequency = 10000.0 ** (-(np.arange(DK) // 2 * 2) / DK)
    sign = np.where(np.arange(DK) % 2 == 0, -1.0, 1.0)
    far = (np.arange(8) * 128.0)[:, None] * frequency[None]
    near = np.arange(128.0)[:, None] * frequency[None]
    table_far = np.stack([np.cos(far), np.sin(far)]).astype(np.float32)
    table_near = np.stack([np.cos(near), np.sin(near)]).astype(np.float32)
    return table_far, table_near, sign.astype(np.float32)[None]


def rms(values, gain):
    scale = lax.rsqrt(jnp.mean(values * values, axis=-1, keepdims=True) + 1e-06)
    return (values * scale * gain).astype(BF16)


def silu(v):
    return v / (1.0 + jnp.exp(-v))


def layer_kernel(
    tok, gain, mlp_gain, decay, length, q, k, v, g, o, fg, fu, far, near, sign,
    res, hid,
    wa, wb, nrm, small, smallw, tokw, wao, wbb, acts, acts2, kv, cosine, sine, qs, gs, runs, column, gated,
    part, got, out_box, rbuf, box,
    sends, za, zb, zr1, zr2, rr, pa1, pa2, pa3, po1, po2, po3, pb1, pb2, pb3, misc, lsem, hsend, hx, hp, hs,
):
    s = Spot()
    post = Post(sends)
    plane_a = PlaneGather(s, post, wao, pl.ds(0, 1536), pa1, pa2, pa3)
    plane_o = PlaneGather(s, post, wao, pl.ds(1536, 512), po1, po2, po3)
    plane_b = PlaneGather(s, post, wbb, pl.ds(0, CB), pb1, pb2, pb3)
    ring1, ring2 = RingGather(s, post, acts, zr1), RingGather(s, post, acts2, zr2)
    barrier = pltpu.get_barrier_semaphore()
    peers = [s.at_z(n)[1] for n in range(1, 8)] + plane_a.neighbours() + [s.partner()]
    for peer in peers:
        pl.semaphore_signal(barrier, inc=1, device_id=peer, device_id_type=MESH)

    for h in range(H):
        wa[h, :, 0:256] = q[:, h * 256 : h * 256 + 256].astype(BF16)
        wa[h, :, 256:512] = k[:, h * 256 : h * 256 + 256].astype(BF16)
        wa[h, :, 512:1024] = v[:, h * 512 : h * 512 + 512].astype(BF16)
        wa[h, :, 1024:1536] = g[:, h * 512 : h * 512 + 512].astype(BF16)
        wa[h, :, 1536:2048] = o[:, h * 512 : h * 512 + 512].astype(BF16)
        wb[h, :, 0:512] = fg[:, h * 512 : h * 512 + 512].astype(BF16)
        wb[h, :, 512:1024] = fu[:, h * 512 : h * 512 + 512].astype(BF16)
    nrm[...] = rms(tok[...].astype(F32), gain[...])
    total = decay[...]
    lane = lax.broadcasted_iota(jnp.int32, (H, SPAN), 1)
    reach = 1
    while reach < SPAN:
        total = total + jnp.where(lane >= reach, pltpu.roll(total, reach, 1), 0.0)
        reach *= 2
    row = lax.broadcasted_iota(jnp.int32, (H, SPAN), 0)
    chosen = jnp.sum(jnp.where(row == s.z, total, 0.0), axis=0, keepdims=True)
    small[...] = jnp.where(row < 4, chosen, length[0, 0])

    pl.semaphore_wait(barrier, len(peers))

    def trade(src, dst, which):
        return pltpu.make_async_remote_copy(
            src_ref=src, dst_ref=dst, send_sem=lsem.at[which], recv_sem=misc.at[which],
            device_id=s.partner(), device_id_type=MESH,
        )

    own_a = local(wa.at[s.z], wao.at[s.dp, s.z, s.xl], lsem.at[0])
    own_b = local(wb.at[s.z], wbb.at[s.dp, s.z, s.xl], lsem.at[3])

    @pl.when(jnp.logical_not(s.same))
    def _():
        trade(nrm, acts.at[slot_of(0)], 1).start()
        trade(tok, tokw, 2).start()

    @pl.when(s.same)
    def _():
        local(nrm, acts.at[slot_of(0)], lsem.at[1])
        local(tok, tokw, lsem.at[2])

    for n in (4, 3, 5, 2, 6, 1, 7):
        zd, peer = s.at_z(n)
        post.send(wa.at[zd], wao.at[s.dp, s.z, s.xl], za.at[n], peer)
    post.send(small, smallw, misc.at[0], s.sibling())

    base = pl.multiple_of(64 * s.c, 64)
    cn, sn = near[0, pl.ds(base, 64)], near[1, pl.ds(base, 64)]
    for i in range(8):
        b, _ = s.at_z(i - 2)
        cf, sf = far[0, pl.ds(b, 1)], far[1, pl.ds(b, 1)]
        cosine[i] = cf * cn - sf * sn
        sine[i] = (sf * cn + cf * sn) * sign[...]

    @pl.when(s.same)
    def _():
        pltpu.make_async_copy(nrm, acts.at[slot_of(0)], lsem.at[1]).wait()

    @pl.when(jnp.logical_not(s.same))
    def _():
        trade(nrm, acts.at[slot_of(0)], 1).wait_recv()

    own_a.wait()
    for n in range(1, 8):
        zs, peer = s.at_z(-n)
        post.arrived(wao.at[s.dp, zs, s.xl], za.at[n], peer)

    plane_a.own()
    ring1.own(0)
    ring1.own(1)

    post.arrived(smallw, misc.at[0], s.sibling())
    runs[...] = jnp.where(s.same, small[...], smallw[...])
    pieces = [runs[0:1, pl.ds(pl.multiple_of(128 * s.at_z(i - 2)[0], 128), 128)] for i in range(8)]
    run_row = jnp.concatenate(pieces, axis=1)
    column[...] = jnp.broadcast_to(run_row, (128, SPAN)).T
    last = runs[4:5, 0:1]
    at = lax.rem(lax.broadcasted_iota(jnp.int32, (1, SPAN), 1) + 128 * (s.z + 6), SPAN)

    plane_a.near_first()
    plane_o.own()
    ring1.step(1, 0)
    ring1.step(1, 1)
    plane_a.far_first()
    plane_a.near_second(0)
    ring1.step(2, 0)
    plane_a.near_second(1)
    plane_o.near_first()
    ring1.step(2, 1)
    plane_a.near_second(2)
    plane_a.far_second(0)
    ring1.step(3, 0)
    plane_o.far_first()
    plane_a.near_second(3)
    plane_a.far_second(1)
    ring1.step(3, 1)
    plane_a.far_second(2)
    plane_a.far_second(3)
    plane_a.from_sibling()

    weights_a = wao.reshape(D, CA)
    weights_b = wbb.reshape(D, CB)

    def project(span, low, width):
        first, count = span
        rows = acts[first : first + count].reshape(64 * count, D)
        return jnp.dot(rows, weights_a[:, low : low + width], preferred_element_type=F32)

    def rot(u, span):
        first, count = span
        n = 64 * count
        even = lax.rem(lax.broadcasted_iota(jnp.int32, (n, DK), 1), 2) == 0
        swapped = jnp.where(even, pltpu.roll(u, DK - 1, 1), pltpu.roll(u, 1, 1))
        turned = u * cosine[first : first + count].reshape(n, DK) + swapped * sine[first : first + count].reshape(n, DK)
        return turned.astype(BF16)

    def key_part(span):
        first, count = span
        kv[first : first + count, s.c, :, 0:256] = rot(project(span, 256, 256), span).reshape(count, 64, 256)

    def value_part(span, which):
        first, count = span
        made = project(span, 512 + 256 * which, 256).astype(BF16).reshape(count, 64, 256)
        kv[first : first + count, s.c, :, 256 + 256 * which : 512 + 256 * which] = made

    def query_part(span):
        first, count = span
        qs[64 * first : 64 * (first + count)] = rot(project(span, 0, 256), span)

    def gate_part(span, which):
        first, count = span
        made = project(span, 1024 + 256 * which, 256).astype(BF16)
        gs[64 * first : 64 * (first + count), 256 * which : 256 * which + 256] = made

    def share(span, arrive):
        mine = kv.at[pl.ds(*span), s.c]
        post.send(mine, mine, arrive, s.sibling())

    def shared(span, arrive):
        post.arrived(kv.at[pl.ds(*span), 1 - s.c], arrive, s.sibling())

    def retain(span):
        first, count = span
        n = 64 * count
        rows = slice(64 * first, 64 * (first + count))
        keys = kv[:, :, :, 0:256].reshape(SPAN, 256)
        values = kv[:, :, :, 256:768].reshape(SPAN, 512)
        scores = lax.dot_general(qs[rows], keys, (((1,), (1,)), ((), ())), preferred_element_type=F32) * (DK**-0.5)
        step = lax.broadcasted_iota(jnp.int32, (n, 1), 0)
        block = lax.div(step, 64)
        place = 128 * lax.rem(block + (s.z + first + 6), 8) + 64 * s.c + (step - 64 * block)
        run_col = jnp.concatenate(
            [column[pl.ds(pl.multiple_of(128 * i + 64 * s.c, 64), 64), 0:1] for i in range(first, first + count)], axis=0
        )
        weights = (scores * jnp.exp(jnp.where(place >= at, run_col - run_row, -jnp.inf))).astype(BF16)
        kept = jnp.dot(weights, values, preferred_element_type=F32)
        mean = jnp.mean(kept, axis=-1, keepdims=True)
        spread = jnp.mean(kept * kept, axis=-1, keepdims=True) - mean * mean
        normed = (kept - mean) * lax.rsqrt(spread + 1e-05)
        live = place.astype(F32) < last
        gated[rows] = jnp.where(live, silu(gs[rows].astype(F32)) * normed, 0.0).astype(BF16)

    def put_out(span):
        first, count = span
        rows = slice(64 * first, 64 * (first + count))
        for tile in range(4):
            wo = weights_a[512 * tile : 512 * tile + 512, 1536:2048]
            made = lax.dot_general(gated[rows], wo, (((1,), (1,)), ((), ())), preferred_element_type=F32)
            part[first : first + count, :, 512 * tile : 512 * tile + 512] = made.astype(BF16).reshape(count, 64, 512)

    key_part(NEAR)
    plane_o.near_second(0)
    value_part(NEAR, 0)
    plane_o.near_second(1)
    value_part(NEAR, 1)
    share(NEAR, misc.at[3])
    ring1.step(4, 0)
    ring1.step(4, 1)
    plane_o.near_second(2)
    plane_o.far_second(0)
    for n in (4, 3, 5, 2, 6, 1, 7):
        zd, peer = s.at_z(n)
        post.send(wb.at[zd], wbb.at[s.dp, s.z, s.xl], zb.at[n], peer)
    key_part(FAR)
    value_part(FAR, 0)
    value_part(FAR, 1)
    share(FAR, misc.at[4])
    plane_o.near_second(3)
    plane_o.far_second(1)
    plane_o.far_second(2)
    query_part(FAR)
    gate_part(FAR, 0)
    gate_part(FAR, 1)
    plane_o.far_second(3)
    shared(NEAR, misc.at[3])
    shared(FAR, misc.at[4])
    retain(FAR)
    plane_o.from_sibling()
    put_out(FAR)

    ways = ((0, 1), (1, -1))

    def rows(half):
        return pl.ds(32 * half, 32)

    def rs_send(way, sign, hop, half, src):
        post.send(src, got.at[way, hop, rows(half)], rr.at[way * 8 + hop * 2 + half], s.at_z(sign)[1])

    def rs_wait(way, sign, hop, half):
        post.arrived(got.at[way, hop, rows(half)], rr.at[way * 8 + hop * 2 + half], s.at_z(-sign)[1])

    def relay(hop, half):
        for way, sign in ways:
            if hop == 1 and half != way:
                continue
            rs_wait(way, sign, hop - 1, half)
            here = part[slot_of((4 - hop) * sign), rows(half)].astype(F32)
            both = here + got[way, hop - 1, rows(half)].astype(F32)
            out_box[way, hop - 1, rows(half)] = both.astype(BF16)
            rs_send(way, sign, hop, half, out_box.at[way, hop - 1, rows(half)])

    for way, sign in ways:
        rs_send(way, sign, 0, way, part.at[slot_of(4), rows(way)])
        rs_send(way, sign, 1, 1 - way, part.at[slot_of(3 * sign), rows(1 - way)])
    own_b.wait()
    for n in range(1, 8):
        zs, peer = s.at_z(-n)
        post.arrived(wbb.at[s.dp, zs, s.xl], zb.at[n], peer)
    plane_b.own()
    query_part(NEAR)
    gate_part(NEAR, 0)
    gate_part(NEAR, 1)
    relay(1, 0)
    relay(1, 1)
    retain(NEAR)
    plane_b.near_first()
    put_out(NEAR)
    relay(2, 1)
    relay(2, 0)
    plane_b.far_first()
    plane_b.near_second(0)
    relay(3, 1)
    relay(3, 0)
    plane_b.near_second(1)
    plane_b.near_second(2)
    plane_b.far_second(0)

    for half in (1, 0):
        for way, sign in ways:
            rs_wait(way, sign, 3, half)
        branch = (
            part[slot_of(0), rows(half)].astype(F32)
            + got[0, 3, rows(half)].astype(F32)
            + got[1, 3, rows(half)].astype(F32)
        )
        residual = (tokw_ready(s, trade, tok, tokw, lsem, half)[rows(half)].astype(F32) + branch).astype(BF16)
        rbuf[rows(half)] = residual
        acts2[slot_of(0), rows(half)] = rms(residual.astype(F32), mlp_gain[...])
        ring2.own(half)

    def hand_back():
        return pltpu.make_async_remote_copy(
            src_ref=rbuf, dst_ref=res, send_sem=lsem.at[4], recv_sem=misc.at[5],
            device_id=s.partner(), device_id_type=MESH,
        )

    @pl.when(s.same)
    def _():
        local(rbuf, res, lsem.at[4])

    @pl.when(jnp.logical_not(s.same))
    def _():
        hand_back().start()

    def hide(span, j, slot):
        first, count = span
        low = pl.multiple_of(256 * j, 256)
        high = pl.multiple_of(256 * j + 512, 256)
        rows2 = acts2[first : first + count].reshape(64 * count, D)
        gate = jnp.dot(rows2, weights_b[:, pl.ds(low, 256)], preferred_element_type=F32)
        up = jnp.dot(rows2, weights_b[:, pl.ds(high, 256)], preferred_element_type=F32)
        box[slot, first : first + count] = (silu(gate) * up).astype(BF16).reshape(count, 64, 256)

    def give(slot, i, peer, arrive):
        b, _ = s.at_z(i - 2)
        return pltpu.make_async_remote_copy(
            src_ref=box.at[slot, i], dst_ref=hid.at[b, s.c], send_sem=hsend.at[8 * slot + i], recv_sem=arrive.at[i],
            device_id=peer, device_id_type=MESH,
        )

    def keep(i):
        b, _ = s.at_z(i - 2)
        return pltpu.make_async_copy(box.at[1, i], hid.at[b, s.c], hsend.at[8 + i])

    def give_far(span):
        first, count = span

        @pl.when(s.same)
        def _():
            for i in range(first, first + count):
                give(0, i, s.across(), hx).start()

        @pl.when(jnp.logical_not(s.same))
        def _():
            for i in range(first, first + count):
                give(0, i, s.partner(), hp).start()

    def give_near(span):
        first, count = span

        @pl.when(s.same)
        def _():
            for i in range(first, first + count):
                keep(i).start()

        @pl.when(jnp.logical_not(s.same))
        def _():
            for i in range(first, first + count):
                give(1, i, s.sibling(), hs).start()

    plane_b.near_second(3)
    plane_b.far_second(1)
    plane_b.far_second(2)
    ring2.step(1, 1)
    ring2.step(1, 0)
    plane_b.far_second(3)
    ring2.step(2, 1)
    ring2.step(2, 0)
    plane_b.from_sibling()
    hide(NEAR, 1 - s.xl, 0)
    give_far(NEAR)
    ring2.step(3, 1)
    ring2.step(3, 0)
    hide(NEAR, s.xl, 1)
    give_near(NEAR)
    ring2.step(4, 1)
    ring2.step(4, 0)
    hide(FAR, 1 - s.xl, 0)
    give_far(FAR)
    hide(FAR, s.xl, 1)
    give_near(FAR)

    @pl.when(s.same)
    def _():
        pltpu.make_async_copy(rbuf, res, lsem.at[4]).wait()
        for i in range(8):
            keep(i).wait()
            give(0, i, s.across(), hx).wait_send()
            b, _ = s.at_z(i - 2)
            post.arrived(hid.at[b, 1 - s.c], hs.at[i], s.sibling())

    @pl.when(jnp.logical_not(s.same))
    def _():
        hand_back().wait()
        trade(nrm, acts.at[slot_of(0)], 1).wait_send()
        trade(tok, tokw, 2).wait_send()
        for i in range(8):
            give(0, i, s.partner(), hp).wait_send()
            give(1, i, s.sibling(), hs).wait_send()
            b, _ = s.at_z(i - 2)
            post.arrived(hid.at[b, s.c], hx.at[i], s.across())
            post.arrived(hid.at[b, 1 - s.c], hp.at[i], s.partner())

    post.finish()


def tokw_ready(s, trade, tok, tokw, lsem, half):
    if half == 1:

        @pl.when(s.same)
        def _():
            pltpu.make_async_copy(tok, tokw, lsem.at[2]).wait()

        @pl.when(jnp.logical_not(s.same))
        def _():
            trade(tok, tokw, 2).wait_recv()

    return tokw


def layer(*args):
    dma = lambda n: pltpu.SemaphoreType.DMA((n,))
    plane_sems = [dma(4), dma(16), dma(16)]
    sends = 7 + 7 + 1 + 2 + 14 + 2 * RingGather.SENDS + 3 * PlaneGather.SENDS
    return pl.pallas_call(
        layer_kernel,
        out_shape=(jax.ShapeDtypeStruct((ROWS, D), BF16), jax.ShapeDtypeStruct((8, 2, ROWS, 256), BF16)),
        in_specs=[VM] * 4 + [SM] + [VM] * 10,
        out_specs=(ANY, ANY),
        scratch_shapes=[
            pltpu.VMEM((8, 8, CA), BF16),
            pltpu.VMEM((8, 8, CB), BF16),
            pltpu.VMEM((ROWS, D), BF16),
            pltpu.VMEM((8, SPAN), F32),
            pltpu.VMEM((8, SPAN), F32),
            pltpu.VMEM((ROWS, D), BF16),
            pltpu.VMEM((16, 8, 2, 8, CA), BF16),
            pltpu.VMEM((16, 8, 2, 8, CB), BF16),
            pltpu.VMEM((8, ROWS, D), BF16),
            pltpu.VMEM((8, ROWS, D), BF16),
            pltpu.VMEM((8, 2, ROWS, 768), BF16),
            pltpu.VMEM((8, ROWS, DK), F32),
            pltpu.VMEM((8, ROWS, DK), F32),
            pltpu.VMEM((512, DK), BF16),
            pltpu.VMEM((512, DV), BF16),
            pltpu.VMEM((8, SPAN), F32),
            pltpu.VMEM((SPAN, 128), F32),
            pltpu.VMEM((512, DV), BF16),
            pltpu.VMEM((8, ROWS, D), BF16),
            pltpu.VMEM((2, 4, ROWS, D), BF16),
            pltpu.VMEM((2, 3, ROWS, D), BF16),
            pltpu.VMEM((ROWS, D), BF16),
            pltpu.VMEM((2, 8, ROWS, 256), BF16),
            dma(sends), dma(8), dma(8), dma(16), dma(16), dma(16),
            *plane_sems, *plane_sems, *plane_sems,
            dma(6), dma(5), dma(16), dma(8), dma(8), dma(8),
        ],
        compiler_params=pltpu.CompilerParams(collective_id=0, has_side_effects=True, vmem_limit_bytes=VMEM_LIMIT),
        name="layer",
    )(*args)


def finish_kernel(res, hid, res_out, hid_out):
    res_out[...] = res[...]
    hid_out[...] = hid[...]


def finish(res, hid):
    return pl.pallas_call(
        finish_kernel,
        out_shape=(jax.ShapeDtypeStruct(res.shape, BF16), jax.ShapeDtypeStruct(hid.shape, BF16)),
        in_specs=[VM] * 2,
        out_specs=(VM, VM),
        name="finish",
    )(res, hid)


def per_device(tokens, norm_gain, mlp_gain, lengths, log_decay, q, k, v, g, o, fg, fu):
    far, near, sign = turn_tables()
    res, hid = layer(
        tokens, norm_gain.reshape(1, D), mlp_gain.reshape(1, D), log_decay.T, lengths.astype(F32).reshape(1, 1),
        q, k, v, g, o.T, fg, fu, far, near, sign,
    )
    return finish(res, hid.reshape(SPAN, 256))


def solution(mesh):
    rows = P(("dp", "mp"), None)
    placed = (rows, P(), P(), P("dp"), P("dp", None), rows, rows, rows, rows, P(None, ("dp", "mp")), rows, rows)
    return jax.shard_map(
        per_device, mesh=mesh, in_specs=placed, out_specs=(rows, P("dp", "mp")), check_vma=False
    )
```

time: 134 us -> 110 us (0.82)
  Pallas kernels: 129 us -> 108 us
  local copies, waits for them, and re-layouts: 3.54 us -> 0 us
    pallas_call x5 -> x2, Pallas kernels: 129 us -> 108 us  [the longest x1 106 us: layer(): pl.pallas_call(layer_kernel, out_shape=(jax.ShapeDtypeStruct((ROWS, D), B...]
    unnamed x2 -> x0, local copies, waits for them, and re-layouts: 3.54 us -> none
where the time goes in v2:
time: 110 us; the launch traced here: 109 us
  Pallas kernels  108 us (98%)
  between operations  1.29 us (1%)
    pallas_call x1, Pallas kernels, layer(): pl.pallas_call(layer_kernel, out_shape=(jax.ShapeDtypeStruct((ROWS, D), B...  106 us

profile of v2, /device:TPU:1, one launch (start us, length us, event | category | flops | bytes accessed | tf_op | source)
XLA Modules:
  0.0 109.0 jit_solution(1794637337537700390)
XLA Ops:
  1.3 105.7 %layer.1 = (bf16[64,2048]{1,0:T(8,128)(2,1)}, bf16[8,2,64,256]{3,2,1,0:T(8,128)(2,1)}) custom-call(bf16[64,2048]{1,0:T(8,128)(2,1)} %tok.1, f32[1,2048]{1,0:T(1,128)} %bitcast.9, f32[1,2048]{1,0:T(1,128)} %bitcast.10, f32[8,1024]{1,0:T(8,128)} %bitcast.8, f32[1,1]{1,0:T(1,128)} %bitcast.3.length, f32[8,2048]{1,0:T(8,128)} %q.1, f32[8,2048]{1,0:T(8,128)} %k.1, ...), custom_call_target="tpu_custom_call" | custom-call | tf_op jit(solution)/shard_map/layer/pallas_call | solution.py:619
  107.0 2.0 %finish.1 = (bf16[64,2048]{1,0:T(8,128)(2,1)}, bf16[1024,256]{1,0:T(8,128)(2,1)}) custom-call(bf16[64,2048]{1,0:T(8,128)(2,1)} %get-tuple-element.4.res, bf16[1024,256]{1,0:T(8,128)(2,1)} %bitcast.6), custom_call_target="tpu_custom_call" | custom-call | tf_op jit(solution)/shard_map/finish/pallas_call | solution.py:663

commit v3 on v2

--- a/solution.py
+++ b/solution.py
@@ -50,85 +50,78 @@
 
 
 class Post:
-    def __init__(self, sends):
-        self.sends, self.count, self.open = sends, 0, []
-
-    def copy(self, src, dst, arrive, peer):
+    def copy(self, src, dst, arrive, peer, done):
         return pltpu.make_async_remote_copy(
-            src_ref=src, dst_ref=dst, send_sem=self.sends.at[self.count], recv_sem=arrive,
-            device_id=peer, device_id_type=MESH,
+            src_ref=src, dst_ref=dst, send_sem=done, recv_sem=arrive, device_id=peer, device_id_type=MESH
         )
 
-    def send(self, src, dst, arrive, peer):
-        made = self.copy(src, dst, arrive, peer)
-        self.count += 1
-        made.start()
-        self.open.append(made)
-
-    def arrived(self, dst, arrive, peer):
-        pltpu.make_async_remote_copy(
-            src_ref=dst, dst_ref=dst, send_sem=self.sends.at[0], recv_sem=arrive,
-            device_id=peer, device_id_type=MESH,
-        ).wait_recv()
-
-    def finish(self):
-        for made in self.open:
-            made.wait_send()
+    def send(self, src, dst, arrive, peer, done):
+        self.copy(src, dst, arrive, peer, done).start()
+
+    def arrived(self, ref, arrive, peer):
+        self.copy(ref, ref, arrive, peer, arrive).wait_recv()
+
+    def sent(self, ref, done, peer):
+        self.copy(ref, ref, done, peer, done).wait_send()
 
 
 class PlaneGather:
-    SENDS, FIRST, SECOND = 4 + 16 + 16, 4, 16
-
-    def __init__(self, spot, post, w, cols, first, second, sib):
-        self.s, self.post, self.w, self.cols = spot, post, w, cols
-        self.first, self.second, self.sib = first, second, sib
-        c = spot.c
-        u, v = (1 - c) * spot.x + c * spot.y, (1 - c) * spot.y + c * spot.x
+    FIRST, SECOND, ENDS = 4, 12, 4
+
+    def __init__(self, spot, post, w, cols, way, first, second, ends):
+        self.s, self.post, self.w, self.cols, self.way = spot, post, w, cols, way
+        self.first, self.second, self.ends = first, second, ends
+        u, v = (spot.y, spot.x) if way else (spot.x, spot.y)
         ring = lambda a, k: lax.rem(a + (k + 4), 4)
         order = (0, -1, 1, 2)
         self.us, self.vs = [ring(u, k) for k in order], [ring(v, k) for k in order]
-        self.sus, self.svs = self.vs, self.us
         self.up, self.um = self.peer(ring(u, 1), v), self.peer(ring(u, -1), v)
         self.vp, self.vm = self.peer(u, ring(v, 1)), self.peer(u, ring(v, -1))
 
-    def xy(self, u, v, c):
-        return (1 - c) * u + c * v, (1 - c) * v + c * u
+    def xy(self, u, v):
+        return (v, u) if self.way else (u, v)
 
     def peer(self, u, v):
-        return self.s.plane(*self.xy(u, v, self.s.c))
-
-    def shard(self, u, v, c, half=None):
-        x, y = self.xy(u, v, c)
-        dp = y * 4 + lax.div(x, 2) * 2 + c
-        rows = pl.ds(0, 8) if half is None else pl.ds(4 * half, 4)
-        return self.w.at[dp, rows, lax.rem(x, 2), :, self.cols]
+        return self.s.plane(*self.xy(u, v))
+
+    def rows(self, half):
+        return pl.ds(4 * self.way, 4) if half is None else pl.ds(4 * self.way + 2 * half, 2)
 
     def mine(self, r, t, half=None):
-        return self.shard(self.us[r], self.vs[t], self.s.c, half)
+        x, y = self.xy(self.us[r], self.vs[t])
+        return self.w.at[y, lax.div(x, 2), self.s.c, self.rows(half), lax.rem(x, 2), :, self.cols]
+
+    def group(self, t):
+        v, c, rows = self.vs[t], self.s.c, self.rows(None)
+        if self.way:
+            return self.w.at[:, lax.div(v, 2), c, rows, lax.rem(v, 2), :, self.cols]
+        return self.w.at[v, :, c, rows, :, :, self.cols]
 
     def neighbours(self):
         return [self.up, self.um, self.vp, self.vm, self.s.sibling()]
 
-    def _go(self, ref, arrive, peer):
-        self.post.send(ref, ref, arrive, peer)
+    def _go(self, ref, arrive, peer, end):
+        self.post.send(ref, ref, arrive, peer, self.ends.at[end])
+
+    def _over(self, ref):
+        self._go(ref, self.ends.at[3], self.s.sibling(), 2)
 
     def own(self):
         ref = self.mine(0, 0)
-        self._go(ref, self.first.at[0], self.up)
-        self._go(ref, self.first.at[1], self.um)
+        self._go(ref, self.first.at[0], self.up, 0)
+        self._go(ref, self.first.at[1], self.um, 0)
         self._row(0)
 
     def _row(self, r):
         ref = self.mine(r, 0)
-        self._go(ref, self.second.at[4 * r], self.vp)
-        self._go(ref, self.second.at[4 * r + 1], self.vm)
-        self._go(ref, self.sib.at[4 * r], self.s.sibling())
+        self._go(ref, self.second.at[3 * r], self.vp, 1)
+        self._go(ref, self.second.at[3 * r + 1], self.vm, 1)
 
     def near_first(self):
         self.post.arrived(self.mine(1, 0), self.first.at[0], self.um)
-        self._go(self.mine(1, 0, 0), self.first.at[2], self.up)
+        self._go(self.mine(1, 0, 0), self.first.at[2], self.up, 0)
         self.post.arrived(self.mine(2, 0), self.first.at[1], self.up)
-        self._go(self.mine(2, 0, 1), self.first.at[3], self.um)
+        self._go(self.mine(2, 0, 1), self.first.at[3], self.um, 0)
         self._row(1)
         self._row(2)
 
@@ -136,25 +129,38 @@
         self.post.arrived(self.mine(3, 0, 0), self.first.at[2], self.um)
         self.post.arrived(self.mine(3, 0, 1), self.first.at[3], self.up)
         self._row(3)
+        self._over(self.group(0))
 
     def near_second(self, r):
-        self.post.arrived(self.mine(r, 1), self.second.at[4 * r], self.vm)
-        self._go(self.mine(r, 1, 0), self.second.at[4 * r + 2], self.vp)
-        self.post.arrived(self.mine(r, 2), self.second.at[4 * r + 1], self.vp)
-        self._go(self.mine(r, 2, 1), self.second.at[4 * r + 3], self.vm)
-        self._go(self.mine(r, 1), self.sib.at[4 * r + 1], self.s.sibling())
-        self._go(self.mine(r, 2), self.sib.at[4 * r + 2], self.s.sibling())
+        self.post.arrived(self.mine(r, 1), self.second.at[3 * r], self.vm)
+        if r < 2:
+            self._go(self.mine(r, 1), self.second.at[3 * r + 2], self.vp, 1)
+        self.post.arrived(self.mine(r, 2), self.second.at[3 * r + 1], self.vp)
+        if r >= 2:
+            self._go(self.mine(r, 2), self.second.at[3 * r + 2], self.vm, 1)
+        if r == 3:
+            self._over(self.group(1))
+            self._over(self.group(2))
 
     def far_second(self, r):
-        self.post.arrived(self.mine(r, 3, 0), self.second.at[4 * r + 2], self.vm)
-        self.post.arrived(self.mine(r, 3, 1), self.second.at[4 * r + 3], self.vp)
-        self._go(self.mine(r, 3), self.sib.at[4 * r + 3], self.s.sibling())
+        self.post.arrived(self.mine(r, 3), self.second.at[3 * r + 2], self.vm if r < 2 else self.vp)
+        self._over(self.mine(r, 3))
 
     def from_sibling(self):
-        for r in range(4):
-            for t in range(4):
-                ref = self.shard(self.sus[r], self.svs[t], 1 - self.s.c)
-                self.post.arrived(ref, self.sib.at[4 * r + t], self.s.sibling())
+        self.post.arrived(self.w.at[0:2, :, :, 0:4, :, :, self.cols], self.ends.at[3], self.s.sibling())
+
+    def finish(self):
+        self.post.sent(self.w.at[0:3, 0, 0, 0:4, 0, :, self.cols], self.ends.at[0], self.up)
+        self.post.sent(self.w.at[0:3, :, 0, 0:4, :, :, self.cols], self.ends.at[1], self.vp)
+        self.post.sent(self.w.at[0:2, :, :, 0:4, :, :, self.cols], self.ends.at[2], self.s.sibling())
+
+
+class Pair:
+    def __init__(self, *parts):
+        self.parts = parts
+
+    def __getattr__(self, name):
+        return lambda *args: [getattr(p, name)(*args) for p in self.parts]
 
 
 def slot_of(r):
@@ -165,29 +171,35 @@
 
 
 class RingGather:
-    SENDS, ARRIVALS = 14, 16
-
-    def __init__(self, spot, post, a, sems):
-        self.s, self.post, self.a, self.sems = spot, post, a, sems
-
-    def part(self, r, half):
-        return self.a.at[slot_of(r), pl.ds(32 * half, 32)]
-
-    def sem(self, way, step, half):
-        return self.sems.at[way * 8 + step * 2 + half]
-
-    def own(self, half):
+    def __init__(self, spot, post, a, sems, count):
+        self.s, self.post, self.a, self.sems, self.done = spot, post, a, sems, sems.at[8 * count]
+        self.count = count
+
+    def part(self, r, i):
+        n = 64 // self.count
+        return self.a.at[slot_of(r), pl.ds(n * i, n)]
+
+    def sem(self, way, step, i):
+        return self.sems.at[(way * 4 + step) * self.count + i]
+
+    def last(self, way, i):
+        return (i < self.count // 2) == (way == 0)
+
+    def own(self, i):
         for way, sign in ((0, 1), (1, -1)):
-            self.post.send(self.part(0, half), self.part(-sign, half), self.sem(way, 0, half), self.s.at_z(sign)[1])
-
-    def step(self, k, half):
+            self.post.send(self.part(0, i), self.part(-sign, i), self.sem(way, 0, i), self.s.at_z(sign)[1], self.done)
+
+    def step(self, k, i):
         for way, sign in ((0, 1), (1, -1)):
-            if k == 4 and half != way:
+            if k == 4 and not self.last(way, i):
                 continue
-            ref = self.part(-sign * k, half)
-            self.post.arrived(ref, self.sem(way, k - 1, half), self.s.at_z(-sign)[1])
-            if k < 3 or (k == 3 and half == way):
-                self.post.send(ref, self.part(-sign * (k + 1), half), self.sem(way, k, half), self.s.at_z(sign)[1])
+            ref = self.part(-sign * k, i)
+            self.post.arrived(ref, self.sem(way, k - 1, i), self.s.at_z(-sign)[1])
+            if k < 3 or (k == 3 and self.last(way, i)):
+                self.post.send(ref, self.part(-sign * (k + 1), i), self.sem(way, k, i), self.s.at_z(sign)[1], self.done)
+
+    def finish(self):
+        self.post.sent(self.a.at[0:7], self.done, self.s.at_z(1)[1])
 
 
 def local(src, dst, sem):
@@ -216,22 +228,34 @@
 
 
 def layer_kernel(
-    tok, gain, mlp_gain, decay, length, q, k, v, g, o, fg, fu, far, near, sign,
+    tok_in, q_in, k_in, v_in, g_in, o_in, fg_in, fu_in, gain, mlp_gain, decay, length, far, near, sign,
     res, hid,
-    wa, wb, nrm, small, smallw, tokw, wao, wbb, acts, acts2, kv, cosine, sine, qs, gs, runs, column, gated,
+    tok, q, k, v, g, o, fg, fu, wa, wb, nrm, small, smallw, tokw, wao, wbb, acts, acts2, kv, cosine, sine, qs, gs, runs, column, gated,
     part, got, out_box, rbuf, box,
-    sends, za, zb, zr1, zr2, rr, pa1, pa2, pa3, po1, po2, po3, pb1, pb2, pb3, misc, lsem, hsend, hx, hp, hs,
+    zsem, zr1, zr2, rr, planes1, planes2, planes3, misc, lsem, hsem, isem,
 ):
     s = Spot()
-    post = Post(sends)
-    plane_a = PlaneGather(s, post, wao, pl.ds(0, 1536), pa1, pa2, pa3)
-    plane_o = PlaneGather(s, post, wao, pl.ds(1536, 512), po1, po2, po3)
-    plane_b = PlaneGather(s, post, wbb, pl.ds(0, CB), pb1, pb2, pb3)
-    ring1, ring2 = RingGather(s, post, acts, zr1), RingGather(s, post, acts2, zr2)
+    post = Post()
+
+    def plane(which, w, cols):
+        return Pair(*[
+            PlaneGather(s, post, w, cols, way, *[p.at[2 * which + way] for p in (planes1, planes2, planes3)])
+            for way in range(2)
+        ])
+
+    plane_a = plane(0, wao, pl.ds(0, 1536))
+    plane_o = plane(1, wao, pl.ds(1536, 512))
+    plane_b = plane(2, wbb, pl.ds(0, CB))
+    ring1, ring2 = RingGather(s, post, acts, zr1, 2), RingGather(s, post, acts2, zr2, 4)
     barrier = pltpu.get_barrier_semaphore()
-    peers = [s.at_z(n)[1] for n in range(1, 8)] + plane_a.neighbours() + [s.partner()]
+    peers = [s.at_z(n)[1] for n in range(1, 8)] + plane_a.parts[0].neighbours() + [s.partner()]
     for peer in peers:
         pl.semaphore_signal(barrier, inc=1, device_id=peer, device_id_type=MESH)
+
+    brought = ((tok_in, tok), (q_in, q), (k_in, k), (v_in, v), (g_in, g), (o_in, o), (fg_in, fg), (fu_in, fu))
+    loads = [local(src, dst, isem.at[n]) for n, (src, dst) in enumerate(brought)]
+    for load in loads:
+        load.wait()
 
     for h in range(H):
         wa[h, :, 0:256] = q[:, h * 256 : h * 256 + 256].astype(BF16)
@@ -260,8 +284,8 @@
             device_id=s.partner(), device_id_type=MESH,
         )
 
-    own_a = local(wa.at[s.z], wao.at[s.dp, s.z, s.xl], lsem.at[0])
-    own_b = local(wb.at[s.z], wbb.at[s.dp, s.z, s.xl], lsem.at[3])
+    own_a = local(wa.at[s.z], wao.at[s.y, s.xh, s.c, s.z, s.xl], lsem.at[0])
+    own_b = local(wb.at[s.z], wbb.at[s.y, s.xh, s.c, s.z, s.xl], lsem.at[3])
 
     @pl.when(jnp.logical_not(s.same))
     def _():
@@ -273,10 +297,13 @@
         local(nrm, acts.at[slot_of(0)], lsem.at[1])
         local(tok, tokw, lsem.at[2])
 
-    for n in (4, 3, 5, 2, 6, 1, 7):
-        zd, peer = s.at_z(n)
-        post.send(wa.at[zd], wao.at[s.dp, s.z, s.xl], za.at[n], peer)
-    post.send(small, smallw, misc.at[0], s.sibling())
+    early, late = pl.ds(0, 1536), pl.ds(1536, 512)
+    for cols, sem in ((early, 0), (late, 4)):
+        for n in (4, 3, 5, 2, 6, 1, 7):
+            zd, peer = s.at_z(n)
+            dst = wao.at[s.y, s.xh, s.c, s.z, s.xl, :, cols]
+            post.send(wa.at[zd, :, cols], dst, zsem.at[sem], peer, zsem.at[sem + 1])
+    post.send(small, smallw, misc.at[0], s.sibling(), misc.at[6])
 
     base = pl.multiple_of(64 * s.c, 64)
     cn, sn = near[0, pl.ds(base, 64)], near[1, pl.ds(base, 64)]
@@ -295,9 +322,7 @@
         trade(nrm, acts.at[slot_of(0)], 1).wait_recv()
 
     own_a.wait()
-    for n in range(1, 8):
-        zs, peer = s.at_z(-n)
-        post.arrived(wao.at[s.dp, zs, s.xl], za.at[n], peer)
+    post.arrived(wao.at[s.y, s.xh, s.c, 0:7, s.xl, :, early], zsem.at[0], s.at_z(1)[1])
 
     plane_a.own()
     ring1.own(0)
@@ -312,6 +337,7 @@
     at = lax.rem(lax.broadcasted_iota(jnp.int32, (1, SPAN), 1) + 128 * (s.z + 6), SPAN)
 
     plane_a.near_first()
+    post.arrived(wao.at[s.y, s.xh, s.c, 0:7, s.xl, :, late], zsem.at[4], s.at_z(1)[1])
     plane_o.own()
     ring1.step(1, 0)
     ring1.step(1, 1)
@@ -319,17 +345,17 @@
     plane_a.near_second(0)
     ring1.step(2, 0)
     plane_a.near_second(1)
-    plane_o.near_first()
     ring1.step(2, 1)
     plane_a.near_second(2)
+    plane_a.near_second(3)
+    plane_o.near_first()
+    ring1.step(3, 0)
     plane_a.far_second(0)
-    ring1.step(3, 0)
-    plane_o.far_first()
-    plane_a.near_second(3)
     plane_a.far_second(1)
     ring1.step(3, 1)
     plane_a.far_second(2)
     plane_a.far_second(3)
+    plane_o.far_first()
     plane_a.from_sibling()
 
     weights_a = wao.reshape(D, CA)
@@ -368,10 +394,10 @@
 
     def share(span, arrive):
         mine = kv.at[pl.ds(*span), s.c]
-        post.send(mine, mine, arrive, s.sibling())
+        post.send(mine, mine, misc.at[arrive], s.sibling(), misc.at[7])
 
     def shared(span, arrive):
-        post.arrived(kv.at[pl.ds(*span), 1 - s.c], arrive, s.sibling())
+        post.arrived(kv.at[pl.ds(*span), 1 - s.c], misc.at[arrive], s.sibling())
 
     def retain(span):
         first, count = span
@@ -403,85 +429,87 @@
             part[first : first + count, :, 512 * tile : 512 * tile + 512] = made.astype(BF16).reshape(count, 64, 512)
 
     key_part(NEAR)
+    value_part(NEAR, 0)
     plane_o.near_second(0)
-    value_part(NEAR, 0)
     plane_o.near_second(1)
     value_part(NEAR, 1)
-    share(NEAR, misc.at[3])
+    share(NEAR, 3)
     ring1.step(4, 0)
     ring1.step(4, 1)
     plane_o.near_second(2)
-    plane_o.far_second(0)
+    plane_o.near_second(3)
     for n in (4, 3, 5, 2, 6, 1, 7):
         zd, peer = s.at_z(n)
-        post.send(wb.at[zd], wbb.at[s.dp, s.z, s.xl], zb.at[n], peer)
+        post.send(wb.at[zd], wbb.at[s.y, s.xh, s.c, s.z, s.xl], zsem.at[2], peer, zsem.at[3])
     key_part(FAR)
     value_part(FAR, 0)
     value_part(FAR, 1)
-    share(FAR, misc.at[4])
-    plane_o.near_second(3)
-    plane_o.far_second(1)
-    plane_o.far_second(2)
+    share(FAR, 4)
     query_part(FAR)
     gate_part(FAR, 0)
     gate_part(FAR, 1)
+    plane_o.far_second(0)
+    plane_o.far_second(1)
+    plane_o.far_second(2)
     plane_o.far_second(3)
-    shared(NEAR, misc.at[3])
-    shared(FAR, misc.at[4])
+    shared(NEAR, 3)
+    shared(FAR, 4)
     retain(FAR)
     plane_o.from_sibling()
     put_out(FAR)
 
     ways = ((0, 1), (1, -1))
 
-    def rows(half):
-        return pl.ds(32 * half, 32)
-
-    def rs_send(way, sign, hop, half, src):
-        post.send(src, got.at[way, hop, rows(half)], rr.at[way * 8 + hop * 2 + half], s.at_z(sign)[1])
-
-    def rs_wait(way, sign, hop, half):
-        post.arrived(got.at[way, hop, rows(half)], rr.at[way * 8 + hop * 2 + half], s.at_z(-sign)[1])
-
-    def relay(hop, half):
-        for way, sign in ways:
-            if hop == 1 and half != way:
-                continue
-            rs_wait(way, sign, hop - 1, half)
-            here = part[slot_of((4 - hop) * sign), rows(half)].astype(F32)
-            both = here + got[way, hop - 1, rows(half)].astype(F32)
-            out_box[way, hop - 1, rows(half)] = both.astype(BF16)
-            rs_send(way, sign, hop, half, out_box.at[way, hop - 1, rows(half)])
+    def rows(i):
+        return pl.ds(16 * i, 16)
+
+    def rs_send(way, hop, i, src):
+        arrive = rr.at[(way * 4 + hop) * 4 + i]
+        post.send(src, got.at[way, hop, rows(i)], arrive, s.at_z(ways[way][1])[1], rr.at[32])
+
+    def rs_wait(way, hop, i):
+        post.arrived(got.at[way, hop, rows(i)], rr.at[(way * 4 + hop) * 4 + i], s.at_z(-ways[way][1])[1])
+
+    def relay(hop, way, i):
+        rs_wait(way, hop - 1, i)
+        here = part[slot_of((4 - hop) * ways[way][1]), rows(i)].astype(F32)
+        both = here + got[way, hop - 1, rows(i)].astype(F32)
+        out_box[way, hop - 1, rows(i)] = both.astype(BF16)
+        rs_send(way, hop, i, out_box.at[way, hop - 1, rows(i)])
+
+    def relay_both(hop, i):
+        for way in range(2):
+            relay(hop, way, i)
 
     for way, sign in ways:
-        rs_send(way, sign, 0, way, part.at[slot_of(4), rows(way)])
-        rs_send(way, sign, 1, 1 - way, part.at[slot_of(3 * sign), rows(1 - way)])
+        for i in (2 * way, 2 * way + 1):
+            rs_send(way, 0, i, part.at[slot_of(4), rows(i)])
+        for i in (2 - 2 * way, 3 - 2 * way):
+            rs_send(way, 1, i, part.at[slot_of(3 * sign), rows(i)])
     own_b.wait()
-    for n in range(1, 8):
-        zs, peer = s.at_z(-n)
-        post.arrived(wbb.at[s.dp, zs, s.xl], zb.at[n], peer)
+    post.arrived(wbb.at[s.y, s.xh, s.c, 0:7, s.xl], zsem.at[2], s.at_z(1)[1])
     plane_b.own()
     query_part(NEAR)
     gate_part(NEAR, 0)
     gate_part(NEAR, 1)
-    relay(1, 0)
-    relay(1, 1)
+    for way, i in ((0, 0), (1, 2), (0, 1), (1, 3)):
+        relay(1, way, i)
     retain(NEAR)
     plane_b.near_first()
     put_out(NEAR)
-    relay(2, 1)
-    relay(2, 0)
+    for i in (2, 0, 3, 1):
+        relay_both(2, i)
     plane_b.far_first()
     plane_b.near_second(0)
-    relay(3, 1)
-    relay(3, 0)
+    for i in (2, 0, 3, 1):
+        relay_both(3, i)
     plane_b.near_second(1)
     plane_b.near_second(2)
     plane_b.far_second(0)
 
-    for half in (1, 0):
-        for way, sign in ways:
-            rs_wait(way, sign, 3, half)
+    for half in (2, 0, 3, 1):
+        for way in range(2):
+            rs_wait(way, 3, half)
         branch = (
             part[slot_of(0), rows(half)].astype(F32)
             + got[0, 3, rows(half)].astype(F32)
@@ -518,13 +546,13 @@
     def give(slot, i, peer, arrive):
         b, _ = s.at_z(i - 2)
         return pltpu.make_async_remote_copy(
-            src_ref=box.at[slot, i], dst_ref=hid.at[b, s.c], send_sem=hsend.at[8 * slot + i], recv_sem=arrive.at[i],
+            src_ref=box.at[slot, i], dst_ref=hid.at[b, s.c], send_sem=hsem.at[slot], recv_sem=hsem.at[arrive],
             device_id=peer, device_id_type=MESH,
         )
 
     def keep(i):
         b, _ = s.at_z(i - 2)
-        return pltpu.make_async_copy(box.at[1, i], hid.at[b, s.c], hsend.at[8 + i])
+        return pltpu.make_async_copy(box.at[1, i], hid.at[b, s.c], hsem.at[1])
 
     def give_far(span):
         first, count = span
@@ -532,12 +560,12 @@
         @pl.when(s.same)
         def _():
             for i in range(first, first + count):
-                give(0, i, s.across(), hx).start()
+                give(0, i, s.across(), 2).start()
 
         @pl.when(jnp.logical_not(s.same))
         def _():
             for i in range(first, first + count):
-                give(0, i, s.partner(), hp).start()
+                give(0, i, s.partner(), 3).start()
 
     def give_near(span):
         first, count = span
@@ -550,25 +578,25 @@
         @pl.when(jnp.logical_not(s.same))
         def _():
             for i in range(first, first + count):
-                give(1, i, s.sibling(), hs).start()
+                give(1, i, s.sibling(), 4).start()
 
     plane_b.near_second(3)
     plane_b.far_second(1)
     plane_b.far_second(2)
-    ring2.step(1, 1)
-    ring2.step(1, 0)
+    for i in (2, 0, 3, 1):
+        ring2.step(1, i)
     plane_b.far_second(3)
-    ring2.step(2, 1)
-    ring2.step(2, 0)
+    for i in (2, 0, 3, 1):
+        ring2.step(2, i)
     plane_b.from_sibling()
     hide(NEAR, 1 - s.xl, 0)
     give_far(NEAR)
-    ring2.step(3, 1)
-    ring2.step(3, 0)
+    for i in (2, 0, 3, 1):
+        ring2.step(3, i)
     hide(NEAR, s.xl, 1)
     give_near(NEAR)
-    ring2.step(4, 1)
-    ring2.step(4, 0)
+    for i in (2, 0, 3, 1):
+        ring2.step(4, i)
     hide(FAR, 1 - s.xl, 0)
     give_far(FAR)
     hide(FAR, s.xl, 1)
@@ -577,29 +605,32 @@
     @pl.when(s.same)
     def _():
         pltpu.make_async_copy(rbuf, res, lsem.at[4]).wait()
-        for i in range(8):
-            keep(i).wait()
-            give(0, i, s.across(), hx).wait_send()
-            b, _ = s.at_z(i - 2)
-            post.arrived(hid.at[b, 1 - s.c], hs.at[i], s.sibling())
+        pltpu.make_async_copy(box.at[1], hid.at[:, s.c], hsem.at[1]).wait()
+        post.sent(box.at[0], hsem.at[0], s.across())
+        post.arrived(hid.at[:, 1 - s.c], hsem.at[4], s.sibling())
 
     @pl.when(jnp.logical_not(s.same))
     def _():
         hand_back().wait()
         trade(nrm, acts.at[slot_of(0)], 1).wait_send()
         trade(tok, tokw, 2).wait_send()
-        for i in range(8):
-            give(0, i, s.partner(), hp).wait_send()
-            give(1, i, s.sibling(), hs).wait_send()
-            b, _ = s.at_z(i - 2)
-            post.arrived(hid.at[b, s.c], hx.at[i], s.across())
-            post.arrived(hid.at[b, 1 - s.c], hp.at[i], s.partner())
-
-    post.finish()
+        post.sent(box.at[0], hsem.at[0], s.partner())
+        post.sent(box.at[1], hsem.at[1], s.sibling())
+        post.arrived(hid.at[:, s.c], hsem.at[2], s.across())
+        post.arrived(hid.at[:, 1 - s.c], hsem.at[3], s.partner())
+
+    post.sent(wa.at[0:7, :, early], zsem.at[1], s.at_z(1)[1])
+    post.sent(wa.at[0:7, :, late], zsem.at[5], s.at_z(1)[1])
+    post.sent(wb.at[0:7], zsem.at[3], s.at_z(1)[1])
+    post.sent(small, misc.at[6], s.sibling())
+    post.sent(kv.at[:, s.c], misc.at[7], s.sibling())
+    post.sent(part.at[0:7], rr.at[32], s.at_z(1)[1])
+    for each in (plane_a, plane_o, plane_b, ring1, ring2):
+        each.finish()
 
 
 def tokw_ready(s, trade, tok, tokw, lsem, half):
-    if half == 1:
+    if half == 2:
 
         @pl.when(s.same)
         def _():
@@ -613,23 +644,23 @@
 
 
 def layer(*args):
-    dma = lambda n: pltpu.SemaphoreType.DMA((n,))
-    plane_sems = [dma(4), dma(16), dma(16)]
-    sends = 7 + 7 + 1 + 2 + 14 + 2 * RingGather.SENDS + 3 * PlaneGather.SENDS
+    dma = lambda *n: pltpu.SemaphoreType.DMA(n)
     return pl.pallas_call(
         layer_kernel,
         out_shape=(jax.ShapeDtypeStruct((ROWS, D), BF16), jax.ShapeDtypeStruct((8, 2, ROWS, 256), BF16)),
-        in_specs=[VM] * 4 + [SM] + [VM] * 10,
+        in_specs=[ANY] * 8 + [VM] * 3 + [SM] + [VM] * 3,
         out_specs=(ANY, ANY),
         scratch_shapes=[
+            pltpu.VMEM((ROWS, D), BF16),
+            *[pltpu.VMEM((8, n), F32) for n in (2048, 2048, 4096, 4096, 4096, 4096, 4096)],
             pltpu.VMEM((8, 8, CA), BF16),
             pltpu.VMEM((8, 8, CB), BF16),
             pltpu.VMEM((ROWS, D), BF16),
             pltpu.VMEM((8, SPAN), F32),
             pltpu.VMEM((8, SPAN), F32),
             pltpu.VMEM((ROWS, D), BF16),
-            pltpu.VMEM((16, 8, 2, 8, CA), BF16),
-            pltpu.VMEM((16, 8, 2, 8, CB), BF16),
+            pltpu.VMEM((4, 2, 2, 8, 2, 8, CA), BF16),
+            pltpu.VMEM((4, 2, 2, 8, 2, 8, CB), BF16),
             pltpu.VMEM((8, ROWS, D), BF16),
             pltpu.VMEM((8, ROWS, D), BF16),
             pltpu.VMEM((8, 2, ROWS, 768), BF16),
@@ -645,9 +676,9 @@
             pltpu.VMEM((2, 3, ROWS, D), BF16),
             pltpu.VMEM((ROWS, D), BF16),
             pltpu.VMEM((2, 8, ROWS, 256), BF16),
-            dma(sends), dma(8), dma(8), dma(16), dma(16), dma(16),
-            *plane_sems, *plane_sems, *plane_sems,
-            dma(6), dma(5), dma(16), dma(8), dma(8), dma(8),
+            dma(6), dma(17), dma(33), dma(33),
+            dma(6, PlaneGather.FIRST), dma(6, PlaneGather.SECOND), dma(6, PlaneGather.ENDS),
+            dma(8), dma(5), dma(5), dma(8),
         ],
         compiler_params=pltpu.CompilerParams(collective_id=0, has_side_effects=True, vmem_limit_bytes=VMEM_LIMIT),
         name="layer",
@@ -672,8 +703,8 @@
 def per_device(tokens, norm_gain, mlp_gain, lengths, log_decay, q, k, v, g, o, fg, fu):
     far, near, sign = turn_tables()
     res, hid = layer(
-        tokens, norm_gain.reshape(1, D), mlp_gain.reshape(1, D), log_decay.T, lengths.astype(F32).reshape(1, 1),
-        q, k, v, g, o.T, fg, fu, far, near, sign,
+        tokens, q, k, v, g, o.T, fg, fu,
+        norm_gain.reshape(1, D), mlp_gain.reshape(1, D), log_decay.T, lengths.astype(F32).reshape(1, 1), far, near, sign,
     )
     return finish(res, hid.reshape(SPAN, 256))
 

time: 110 us -> 102 us (0.927)
  Pallas kernels: 108 us -> 100 us
    pallas_call x1, Pallas kernels: 106 us -> 98.2 us  [layer(): pl.pallas_call(layer_kernel, out_shape=(jax.ShapeDtypeStruct((ROWS, D), B...]
where the time goes in v3:
time: 102 us; the launch traced here: 101 us
  Pallas kernels  100 us (98%)
  between operations  1.29 us (1%)
    pallas_call x1, Pallas kernels, layer(): pl.pallas_call(layer_kernel, out_shape=(jax.ShapeDtypeStruct((ROWS, D), B...  98.2 us

profile of v3, /device:TPU:1, one launch (start us, length us, event | category | flops | bytes accessed | tf_op | source)
XLA Modules:
  0.0 101.5 jit_solution(15437160057339002165)
XLA Ops:
  1.3 98.2 %layer.1 = (bf16[64,2048]{1,0:T(8,128)(2,1)}, bf16[8,2,64,256]{3,2,1,0:T(8,128)(2,1)}) custom-call(bf16[64,2048]{1,0:T(8,128)(2,1)} %tok_in.1, f32[8,2048]{1,0:T(8,128)} %q_in.1, f32[8,2048]{1,0:T(8,128)} %k_in.1, f32[8,4096]{1,0:T(8,128)} %v_in.1, f32[8,4096]{1,0:T(8,128)} %g_in.1, f32[8,4096]{1,0:T(8,128)} %bitcast.7, f32[8,4096]{1,0:T(8,128)} %fg_in.1, ...), custom_call_target="tpu_custom_call" | custom-call | tf_op jit(solution)/shard_map/layer/pallas_call | solution.py:648
  99.5 2.0 %finish.1 = (bf16[64,2048]{1,0:T(8,128)(2,1)}, bf16[1024,256]{1,0:T(8,128)(2,1)}) custom-call(bf16[64,2048]{1,0:T(8,128)(2,1)} %get-tuple-element.4.res, bf16[1024,256]{1,0:T(8,128)(2,1)} %bitcast.6), custom_call_target="tpu_custom_call" | custom-call | tf_op jit(solution)/shard_map/finish/pallas_call | solution.py:694

commit v4 on v3

--- a/solution.py
+++ b/solution.py
@@ -106,10 +106,12 @@
     def _over(self, ref):
         self._go(ref, self.ends.at[3], self.s.sibling(), 2)
 
-    def own(self):
+    def own_first(self):
         ref = self.mine(0, 0)
         self._go(ref, self.first.at[0], self.up, 0)
         self._go(ref, self.first.at[1], self.um, 0)
+
+    def own_row(self):
         self._row(0)
 
     def _row(self, r):
@@ -122,6 +124,8 @@
         self._go(self.mine(1, 0, 0), self.first.at[2], self.up, 0)
         self.post.arrived(self.mine(2, 0), self.first.at[1], self.up)
         self._go(self.mine(2, 0, 1), self.first.at[3], self.um, 0)
+
+    def near_rows(self):
         self._row(1)
         self._row(2)
 
@@ -324,7 +328,8 @@
     own_a.wait()
     post.arrived(wao.at[s.y, s.xh, s.c, 0:7, s.xl, :, early], zsem.at[0], s.at_z(1)[1])
 
-    plane_a.own()
+    plane_a.own_first()
+    plane_a.own_row()
     ring1.own(0)
     ring1.own(1)
 
@@ -336,19 +341,22 @@
     last = runs[4:5, 0:1]
     at = lax.rem(lax.broadcasted_iota(jnp.int32, (1, SPAN), 1) + 128 * (s.z + 6), SPAN)
 
+    post.arrived(wao.at[s.y, s.xh, s.c, 0:7, s.xl, :, late], zsem.at[4], s.at_z(1)[1])
+    plane_o.own_first()
     plane_a.near_first()
-    post.arrived(wao.at[s.y, s.xh, s.c, 0:7, s.xl, :, late], zsem.at[4], s.at_z(1)[1])
-    plane_o.own()
+    plane_a.near_rows()
     ring1.step(1, 0)
     ring1.step(1, 1)
     plane_a.far_first()
+    plane_o.near_first()
+    plane_o.own_row()
     plane_a.near_second(0)
     ring1.step(2, 0)
     plane_a.near_second(1)
     ring1.step(2, 1)
     plane_a.near_second(2)
     plane_a.near_second(3)
-    plane_o.near_first()
+    plane_o.near_rows()
     ring1.step(3, 0)
     plane_a.far_second(0)
     plane_a.far_second(1)
@@ -488,7 +496,8 @@
             rs_send(way, 1, i, part.at[slot_of(3 * sign), rows(i)])
     own_b.wait()
     post.arrived(wbb.at[s.y, s.xh, s.c, 0:7, s.xl], zsem.at[2], s.at_z(1)[1])
-    plane_b.own()
+    plane_b.own_first()
+    plane_b.own_row()
     query_part(NEAR)
     gate_part(NEAR, 0)
     gate_part(NEAR, 1)
@@ -496,6 +505,7 @@
         relay(1, way, i)
     retain(NEAR)
     plane_b.near_first()
+    plane_b.near_rows()
     put_out(NEAR)
     for i in (2, 0, 3, 1):
         relay_both(2, i)
@@ -534,14 +544,15 @@
     def _():
         hand_back().start()
 
-    def hide(span, j, slot):
-        first, count = span
+    def hide(slots, j, slot):
         low = pl.multiple_of(256 * j, 256)
         high = pl.multiple_of(256 * j + 512, 256)
-        rows2 = acts2[first : first + count].reshape(64 * count, D)
+        rows2 = jnp.concatenate([acts2[i] for i in slots], axis=0)
         gate = jnp.dot(rows2, weights_b[:, pl.ds(low, 256)], preferred_element_type=F32)
         up = jnp.dot(rows2, weights_b[:, pl.ds(high, 256)], preferred_element_type=F32)
-        box[slot, first : first + count] = (silu(gate) * up).astype(BF16).reshape(count, 64, 256)
+        made = (silu(gate) * up).astype(BF16)
+        for n, i in enumerate(slots):
+            box[slot, i] = made[64 * n : 64 * n + 64]
 
     def give(slot, i, peer, arrive):
         b, _ = s.at_z(i - 2)
@@ -554,30 +565,26 @@
         b, _ = s.at_z(i - 2)
         return pltpu.make_async_copy(box.at[1, i], hid.at[b, s.c], hsem.at[1])
 
-    def give_far(span):
-        first, count = span
-
+    def give_far(slots):
         @pl.when(s.same)
         def _():
-            for i in range(first, first + count):
+            for i in slots:
                 give(0, i, s.across(), 2).start()
 
         @pl.when(jnp.logical_not(s.same))
         def _():
-            for i in range(first, first + count):
+            for i in slots:
                 give(0, i, s.partner(), 3).start()
 
-    def give_near(span):
-        first, count = span
-
+    def give_near(slots):
         @pl.when(s.same)
         def _():
-            for i in range(first, first + count):
+            for i in slots:
                 keep(i).start()
 
         @pl.when(jnp.logical_not(s.same))
         def _():
-            for i in range(first, first + count):
+            for i in slots:
                 give(1, i, s.sibling(), 4).start()
 
     plane_b.near_second(3)
@@ -589,18 +596,20 @@
     for i in (2, 0, 3, 1):
         ring2.step(2, i)
     plane_b.from_sibling()
-    hide(NEAR, 1 - s.xl, 0)
-    give_far(NEAR)
+    hide(range(0, 5), 1 - s.xl, 0)
+    give_far(range(0, 5))
     for i in (2, 0, 3, 1):
         ring2.step(3, i)
-    hide(NEAR, s.xl, 1)
-    give_near(NEAR)
+    hide((5, 7), 1 - s.xl, 0)
+    give_far((5, 7))
+    hide(range(0, 5), s.xl, 1)
+    give_near(range(0, 5))
     for i in (2, 0, 3, 1):
         ring2.step(4, i)
-    hide(FAR, 1 - s.xl, 0)
-    give_far(FAR)
-    hide(FAR, s.xl, 1)
-    give_near(FAR)
+    hide((6,), 1 - s.xl, 0)
+    give_far((6,))
+    hide((5, 6, 7), s.xl, 1)
+    give_near((5, 6, 7))
 
     @pl.when(s.same)
     def _():

time: 102 us -> 99.3 us (0.974)
  Pallas kernels: 100 us -> 97.8 us
    pallas_call x1, Pallas kernels: 98.2 us -> 95.8 us  [layer(): pl.pallas_call(layer_kernel, out_shape=(jax.ShapeDtypeStruct((ROWS, D), B...]
where the time goes in v4:
time: 99.3 us; the launch traced here: 99.1 us
  Pallas kernels  97.8 us (98%)
  between operations  1.29 us (1%)
    pallas_call x1, Pallas kernels, layer(): pl.pallas_call(layer_kernel, out_shape=(jax.ShapeDtypeStruct((ROWS, D), B...  95.8 us
    pallas_call x1, Pallas kernels, finish(): pl.pallas_call(finish_kernel, out_shape=(jax.ShapeDtypeStruct(res.shape,...  2.02 us

profile of v4, /device:TPU:1, one launch (start us, length us, event | category | flops | bytes accessed | tf_op | source)
XLA Modules:
  0.0 99.1 jit_solution(15842405037705646779)
XLA Ops:
  1.3 95.8 %layer.1 = (bf16[64,2048]{1,0:T(8,128)(2,1)}, bf16[8,2,64,256]{3,2,1,0:T(8,128)(2,1)}) custom-call(bf16[64,2048]{1,0:T(8,128)(2,1)} %tok_in.1, f32[8,2048]{1,0:T(8,128)} %q_in.1, f32[8,2048]{1,0:T(8,128)} %k_in.1, f32[8,4096]{1,0:T(8,128)} %v_in.1, f32[8,4096]{1,0:T(8,128)} %g_in.1, f32[8,4096]{1,0:T(8,128)} %bitcast.7, f32[8,4096]{1,0:T(8,128)} %fg_in.1, ...), custom_call_target="tpu_custom_call" | custom-call | tf_op jit(solution)/shard_map/layer/pallas_call | solution.py:657
  97.1 2.0 %finish.1 = (bf16[64,2048]{1,0:T(8,128)(2,1)}, bf16[1024,256]{1,0:T(8,128)(2,1)}) custom-call(bf16[64,2048]{1,0:T(8,128)(2,1)} %get-tuple-element.4.res, bf16[1024,256]{1,0:T(8,128)(2,1)} %bitcast.6), custom_call_target="tpu_custom_call" | custom-call | tf_op jit(solution)/shard_map/finish/pallas_call | solution.py:703

commit v5 on v4

--- a/solution.py
+++ b/solution.py
@@ -694,17 +694,30 @@
     )(*args)
 
 
-def finish_kernel(res, hid, res_out, hid_out):
-    res_out[...] = res[...]
-    hid_out[...] = hid[...]
+def finish_kernel(res, hid, res_out, hid_out, res_box, hid_box, into, outof):
+    quarters = [pl.ds(256 * n, 256) for n in range(4)]
+    steps = [(res, res_box, res_out)] + [(hid.at[r], hid_box.at[r], hid_out.at[r]) for r in quarters]
+    loads = [local(src, box, into.at[n]) for n, (src, box, _) in enumerate(steps)]
+    stores = []
+    for n, (_, box, dst) in enumerate(steps):
+        loads[n].wait()
+        stores.append(local(box, dst, outof.at[n]))
+    for store in stores:
+        store.wait()
 
 
 def finish(res, hid):
     return pl.pallas_call(
         finish_kernel,
         out_shape=(jax.ShapeDtypeStruct(res.shape, BF16), jax.ShapeDtypeStruct(hid.shape, BF16)),
-        in_specs=[VM] * 2,
-        out_specs=(VM, VM),
+        in_specs=[ANY] * 2,
+        out_specs=(ANY, ANY),
+        scratch_shapes=[
+            pltpu.VMEM(res.shape, BF16),
+            pltpu.VMEM(hid.shape, BF16),
+            pltpu.SemaphoreType.DMA((5,)),
+            pltpu.SemaphoreType.DMA((5,)),
+        ],
         name="finish",
     )(res, hid)
 

time: 99.3 us -> 99.2 us (level)
  no operation moved by 1% of the time
where the time goes in v5:
time: 99.2 us; the launch traced here: 99 us
  Pallas kernels  97.7 us (98%)
  between operations  1.29 us (1%)
    pallas_call x1, Pallas kernels, layer(): pl.pallas_call(layer_kernel, out_shape=(jax.ShapeDtypeStruct((ROWS, D), B...  95.8 us

profile of v5, /device:TPU:1, one launch (start us, length us, event | category | flops | bytes accessed | tf_op | source)
XLA Modules:
  0.0 99.0 jit_solution(408052175285480362)
XLA Ops:
  1.3 95.8 %layer.1 = (bf16[64,2048]{1,0:T(8,128)(2,1)}, bf16[8,2,64,256]{3,2,1,0:T(8,128)(2,1)}) custom-call(bf16[64,2048]{1,0:T(8,128)(2,1)} %tok_in.1, f32[8,2048]{1,0:T(8,128)} %q_in.1, f32[8,2048]{1,0:T(8,128)} %k_in.1, f32[8,4096]{1,0:T(8,128)} %v_in.1, f32[8,4096]{1,0:T(8,128)} %g_in.1, f32[8,4096]{1,0:T(8,128)} %bitcast.7, f32[8,4096]{1,0:T(8,128)} %fg_in.1, ...), custom_call_target="tpu_custom_call" | custom-call | tf_op jit(solution)/shard_map/layer/pallas_call | solution.py:657
  97.1 1.9 %finish.1 = (bf16[64,2048]{1,0:T(8,128)(2,1)}, bf16[1024,256]{1,0:T(8,128)(2,1)}) custom-call(bf16[64,2048]{1,0:T(8,128)(2,1)} %get-tuple-element.4.res, bf16[1024,256]{1,0:T(8,128)(2,1)} %bitcast.6), custom_call_target="tpu_custom_call" | custom-call | tf_op jit(solution)/shard_map/finish/pallas_call | solution.py:710
